TPU v7x, 32 devices: a whole 2x2x4 slice. The times are simulated.
32 devices in a mesh: rep: 4 (over y, x), fsdp: 8 (over z, core).
Axes of the slice: x: 2, y: 2, z: 4, core: 2. Of those that a mesh axis runs over, the one named last changes fastest.
Arguments:
- patches: bfloat16 [128, 128, 1024], P(('rep', 'fsdp')), may hold values from -6 to 6
- enc_gain1: bfloat16 [1024], P('fsdp'), may hold values from 0.5 to 1.5
- enc_qkv: bfloat16 [1024, 3072], P('fsdp'), may hold values from -0.1875 to 0.1875
- enc_proj: bfloat16 [1024, 1024], P('fsdp'), may hold values from -1.5 to 1.5
- enc_gain2: bfloat16 [1024], P('fsdp'), may hold values from 0.5 to 1.5
- enc_up: bfloat16 [1024, 4096], P('fsdp'), may hold values from -0.1875 to 0.1875
- enc_down: bfloat16 [4096, 1024], P('fsdp'), may hold values from -0.09375 to 0.09375
- embed_w: bfloat16 [1024, 512], P('fsdp'), may hold values from -0.1875 to 0.1875
- mask_token: bfloat16 [512], P('fsdp'), may hold values from -6 to 6
- dec_gain1: bfloat16 [512], P('fsdp'), may hold values from 0.5 to 1.5
- dec_qkv: bfloat16 [512, 1536], P('fsdp'), may hold values from -0.25 to 0.25
- dec_proj: bfloat16 [512, 512], P('fsdp'), may hold values from -2 to 2
- dec_gain2: bfloat16 [512], P('fsdp'), may hold values from 0.5 to 1.5
- dec_up: bfloat16 [512, 2048], P('fsdp'), may hold values from -0.25 to 0.25
- dec_down: bfloat16 [2048, 512], P('fsdp'), may hold values from -0.125 to 0.125
- visible: int32 [128], P(('rep', 'fsdp')), may hold values from 64 to 128, as said below
- unshuffle: int32 [128, 256], P(('rep', 'fsdp')), may hold values from 0 to 255, each once within a row
- ground_dist: float32 [128], P(('rep', 'fsdp')), may hold values from 0.5 to 2
- cotangent: bfloat16 [128, 256, 512], P(('rep', 'fsdp')), may hold values from -6 to 6
Outputs:
- enc_out: bfloat16 [128, 128, 1024], P(('rep', 'fsdp'))
- dec_out: bfloat16 [128, 256, 512], P(('rep', 'fsdp'))
- patches_grad: bfloat16 [128, 128, 1024], P(('rep', 'fsdp'))
- grad_enc_gain1: float32 [1024], P('fsdp')
- grad_enc_qkv: float32 [1024, 3072], P('fsdp')
- grad_enc_proj: float32 [1024, 1024], P('fsdp')
- grad_enc_gain2: float32 [1024], P('fsdp')
- grad_enc_up: float32 [1024, 4096], P('fsdp')
- grad_enc_down: float32 [4096, 1024], P('fsdp')
- grad_embed: float32 [1024, 512], P('fsdp')
- grad_mask: float32 [512], P('fsdp')
- grad_dec_gain1: float32 [512], P('fsdp')
- grad_dec_qkv: float32 [512, 1536], P('fsdp')
- grad_dec_proj: float32 [512, 512], P('fsdp')
- grad_dec_gain2: float32 [512], P('fsdp')
- grad_dec_up: float32 [512, 2048], P('fsdp')
- grad_dec_down: float32 [2048, 512], P('fsdp')
Inputs may be any that keep to these rules, and one draw needn't show every extreme that they name: The first visible[i] encoder slots of image i are live, the rest are padding; some image has 128 live slots and some 128 // 2. `unshuffle`: each row is a permutation of 0 to 255.
All inputs are finite; a program needn't handle non-finite values.
Results may differ from a plain program's by a relative error of at most 0.024.
Values may be sent and summed in bfloat16 or wider, within the bound.
A program may use at most 256 MiB of HBM per device.

v0:
```python
import math

import jax
import jax.numpy as jnp
from jax import lax
from jax.sharding import PartitionSpec as P

HEADS = 16
HEADS_D = 16
GRID = 16


norm_epsilon = 1e-06


def matmul(left, right):
    return jnp.dot(left, right, preferred_element_type=jnp.float32)


def matmul_tn(left, right):
    return lax.dot_general(
        left, right, (((0,), (0,)), ((), ())), preferred_element_type=jnp.float32
    )


def matmul_nt(left, right):
    return lax.dot_general(
        left, right, (((1,), (1,)), ((), ())), preferred_element_type=jnp.float32
    )


def norm_stats(values):
    centre = values - jnp.mean(values, axis=-1, keepdims=True)
    inv_dev = lax.rsqrt(jnp.mean(centre * centre, axis=-1, keepdims=True) + norm_epsilon)
    return (centre * inv_dev, inv_dev)


def norm_back(d_scaled, normal, inv_dev):
    return inv_dev * (
        d_scaled
        - jnp.mean(d_scaled, axis=-1, keepdims=True)
        - normal * jnp.mean(d_scaled * normal, axis=-1, keepdims=True)
    )


def position_table(distance, grid_side, model_width):
    quarter = model_width // 4
    frequency = 1.0 / 10000.0 ** (jnp.arange(quarter, dtype=jnp.float32) / quarter)
    places = jnp.arange(grid_side * grid_side, dtype=jnp.int32)
    column = (places % grid_side).astype(jnp.float32)
    row_pos = (places // grid_side).astype(jnp.float32)
    along_c = distance[:, None, None] * column[None, :, None] * frequency[None, None, :]
    along_r = distance[:, None, None] * row_pos[None, :, None] * frequency[None, None, :]
    return jnp.concatenate(
        [jnp.sin(along_c), jnp.cos(along_c), jnp.sin(along_r), jnp.cos(along_r)], axis=-1
    )


def by_groups(function, members, length):
    images = members[0].shape[0]
    per_step = math.gcd(images, max(1, 512 // length))
    shaped = tuple(
        (member.reshape((images // per_step, per_step) + member.shape[1:]) for member in members)
    )
    results = lax.map(lambda group_items: function(*group_items), shaped)
    return jax.tree.map(lambda result: result.reshape((images,) + result.shape[2:]), results)


def masked_scores(queries, key_rows, live, score_scale):
    raw_scores = (
        jnp.einsum("nqhd,nkhd->nhqk", queries, key_rows, preferred_element_type=jnp.float32)
        * score_scale
    )
    length = key_rows.shape[1]
    valid = jnp.arange(length, dtype=jnp.int32)[None, None, None, :] < live[:, None, None, None]
    return jnp.where(valid, raw_scores, -1e30)


def split_heads(packed, head_count):
    images, length, three_width = packed.shape
    split_parts = packed.reshape(images, length, 3, head_count, three_width // (3 * head_count))
    return (split_parts[:, :, 0], split_parts[:, :, 1], split_parts[:, :, 2])


def attend_group(packed, live, head_count, score_scale):
    queries, key_rows, value_rows = split_heads(packed, head_count)
    scores = masked_scores(queries, key_rows, live, score_scale)
    highest = jnp.max(scores, axis=-1, keepdims=True)
    exponent = jnp.exp(scores - highest)
    summed = jnp.sum(exponent, axis=-1, keepdims=True)
    soft_weights = (exponent / summed).astype(jnp.bfloat16)
    mixed_rows = jnp.einsum(
        "nhqk,nkhd->nqhd", soft_weights, value_rows, preferred_element_type=jnp.float32
    )
    images, length = (packed.shape[0], packed.shape[1])
    log_total = (highest + jnp.log(summed))[..., 0]
    return (
        mixed_rows.reshape(images, length, packed.shape[2] // 3).astype(jnp.bfloat16),
        log_total,
    )


def attend_back_group(packed, log_total, d_mixed, live, head_count, score_scale):
    queries, key_rows, value_rows = split_heads(packed, head_count)
    scores = masked_scores(queries, key_rows, live, score_scale)
    soft_float = jnp.exp(scores - log_total[..., None])
    d_heads = d_mixed.reshape(queries.shape)
    d_soft = jnp.einsum("nqhd,nkhd->nhqk", d_heads, value_rows, preferred_element_type=jnp.float32)
    row_dot = jnp.sum(soft_float * d_soft, axis=-1, keepdims=True)
    d_scores = (soft_float * (d_soft - row_dot)).astype(jnp.bfloat16)
    d_queries = (
        jnp.einsum("nhqk,nkhd->nqhd", d_scores, key_rows, preferred_element_type=jnp.float32)
        * score_scale
    )
    d_keys = (
        jnp.einsum("nhqk,nqhd->nkhd", d_scores, queries, preferred_element_type=jnp.float32)
        * score_scale
    )
    d_values = jnp.einsum(
        "nhqk,nqhd->nkhd",
        soft_float.astype(jnp.bfloat16),
        d_heads,
        preferred_element_type=jnp.float32,
    )
    stacked = jnp.stack([d_queries, d_keys, d_values], axis=2)
    return stacked.reshape(packed.shape).astype(jnp.bfloat16)


def block_forward(rows, weights, live, head_count, images, length):
    gain_one, w_qkv, w_out, gain_two, w_up, w_down = weights
    model_width = rows.shape[-1]
    score_scale = (model_width // head_count) ** (-0.5)
    normal_one, inv_one = norm_stats(rows)
    normed_one = (normal_one * gain_one).astype(jnp.bfloat16)
    packed = matmul(normed_one, w_qkv).astype(jnp.bfloat16).reshape(images, length, 3 * model_width)

    def attend(group_packed, group_live):
        return attend_group(group_packed, group_live, head_count, score_scale)

    mixed_rows, log_total = by_groups(attend, (packed, live), length)
    middle = rows + matmul(mixed_rows.reshape(images * length, model_width), w_out)
    normal_two, inv_two = norm_stats(middle)
    normed_two = (normal_two * gain_two).astype(jnp.bfloat16)
    hidden = jax.nn.gelu(matmul(normed_two, w_up), approximate=False).astype(jnp.bfloat16)
    return (middle + matmul(hidden, w_down), (rows, packed, mixed_rows, log_total, middle))


def block_backward(kept_state, d_out, weights, live, head_count, images, length):
    rows, packed, mixed_rows, log_total, middle = kept_state
    gain_one, w_qkv, w_out, gain_two, w_up, w_down = weights
    model_width = rows.shape[-1]
    score_scale = (model_width // head_count) ** (-0.5)
    normal_two, inv_two = norm_stats(middle)
    normed_two = (normal_two * gain_two).astype(jnp.bfloat16)
    up_proj = matmul(normed_two, w_up)
    hidden_float, gelu_back = jax.vjp(lambda inner: jax.nn.gelu(inner, approximate=False), up_proj)
    hidden = hidden_float.astype(jnp.bfloat16)
    d_branch = d_out.astype(jnp.bfloat16)
    grad_down = matmul_tn(hidden, d_branch)
    d_hidden = matmul_nt(d_branch, w_down)
    d_up = gelu_back(d_hidden)[0].astype(jnp.bfloat16)
    grad_up = matmul_tn(normed_two, d_up)
    d_normed_two = matmul_nt(d_up, w_up)
    grad_gain_two = jnp.sum(d_normed_two * normal_two, axis=0)
    d_middle = d_out + norm_back(d_normed_two * gain_two, normal_two, inv_two)
    d_attn = d_middle.astype(jnp.bfloat16)
    grad_out = matmul_tn(mixed_rows.reshape(images * length, model_width), d_attn)
    d_mixed = matmul_nt(d_attn, w_out).astype(jnp.bfloat16).reshape(images, length, model_width)

    def attend_back(group_packed, group_total, group_grad, group_live):
        return attend_back_group(
            group_packed, group_total, group_grad, group_live, head_count, score_scale
        )

    d_packed = by_groups(attend_back, (packed, log_total, d_mixed, live), length)
    d_packed = d_packed.reshape(images * length, 3 * model_width)
    normal_one, inv_one = norm_stats(rows)
    normed_one = (normal_one * gain_one).astype(jnp.bfloat16)
    grad_qkv = matmul_tn(normed_one, d_packed)
    d_normed_one = matmul_nt(d_packed, w_qkv)
    grad_gain_one = jnp.sum(d_normed_one * normal_one, axis=0)
    d_rows = d_middle + norm_back(d_normed_one * gain_one, normal_one, inv_one)
    return (d_rows, (grad_gain_one, grad_qkv, grad_out, grad_gain_two, grad_up, grad_down))


def shards(
    patches,
    enc_gain1,
    enc_qkv,
    enc_proj,
    enc_gain2,
    enc_up,
    enc_down,
    embed_w,
    mask_token,
    dec_gain1,
    dec_qkv,
    dec_proj,
    dec_gain2,
    dec_up,
    dec_down,
    visible,
    unshuffle,
    ground_dist,
    cotangent,
):
    images, slot_count, model_width = patches.shape
    patch_count = unshuffle.shape[1]
    dec_width = embed_w.shape[1]
    enc_full = (
        lax.all_gather(enc_gain1, "fsdp", axis=0, tiled=True),
        lax.all_gather(enc_qkv, "fsdp", axis=0, tiled=True),
        lax.all_gather(enc_proj, "fsdp", axis=0, tiled=True),
        lax.all_gather(enc_gain2, "fsdp", axis=0, tiled=True),
        lax.all_gather(enc_up, "fsdp", axis=0, tiled=True),
        lax.all_gather(enc_down, "fsdp", axis=0, tiled=True),
    )
    rows_in = patches.astype(jnp.float32).reshape(images * slot_count, model_width)
    enc_rows, enc_state = block_forward(rows_in, enc_full, visible, HEADS, images, slot_count)
    dec_full = (
        lax.all_gather(embed_w, "fsdp", axis=0, tiled=True),
        lax.all_gather(mask_token, "fsdp", axis=0, tiled=True),
        lax.all_gather(dec_gain1, "fsdp", axis=0, tiled=True),
        lax.all_gather(dec_qkv, "fsdp", axis=0, tiled=True),
        lax.all_gather(dec_proj, "fsdp", axis=0, tiled=True),
        lax.all_gather(dec_gain2, "fsdp", axis=0, tiled=True),
        lax.all_gather(dec_up, "fsdp", axis=0, tiled=True),
        lax.all_gather(dec_down, "fsdp", axis=0, tiled=True),
    )
    enc_low = enc_rows.astype(jnp.bfloat16)
    embedded = matmul(enc_low, dec_full[0]).reshape(images, slot_count, dec_width)
    picked = jnp.take_along_axis(
        embedded, jnp.minimum(unshuffle, slot_count - 1)[:, :, None], axis=1
    )
    shown_rows = (unshuffle < visible[:, None])[:, :, None]
    dec_in = jnp.where(
        shown_rows, picked, dec_full[1].astype(jnp.float32)[None, None, :]
    ) + position_table(ground_dist, GRID, dec_width)
    all_live = jnp.full((images,), patch_count, jnp.int32)
    dec_rows, dec_state = block_forward(
        dec_in.reshape(images * patch_count, dec_width),
        dec_full[2:],
        all_live,
        HEADS_D,
        images,
        patch_count,
    )
    dec_again = (
        lax.all_gather(embed_w, "fsdp", axis=0, tiled=True),
        lax.all_gather(mask_token, "fsdp", axis=0, tiled=True),
        lax.all_gather(dec_gain1, "fsdp", axis=0, tiled=True),
        lax.all_gather(dec_qkv, "fsdp", axis=0, tiled=True),
        lax.all_gather(dec_proj, "fsdp", axis=0, tiled=True),
        lax.all_gather(dec_gain2, "fsdp", axis=0, tiled=True),
        lax.all_gather(dec_up, "fsdp", axis=0, tiled=True),
        lax.all_gather(dec_down, "fsdp", axis=0, tiled=True),
    )
    d_dec = cotangent.astype(jnp.float32).reshape(images * patch_count, dec_width)
    d_dec_in, dec_grads = block_backward(
        dec_state, d_dec, dec_again[2:], all_live, HEADS_D, images, patch_count
    )
    d_positions = d_dec_in.reshape(images, patch_count, dec_width)
    grad_mask = jnp.sum(jnp.where(shown_rows, 0.0, d_positions), axis=(0, 1))
    inverse = jnp.argsort(unshuffle, axis=1)[:, :slot_count]
    slot_live = (jnp.arange(slot_count, dtype=jnp.int32)[None, :] < visible[:, None])[:, :, None]
    d_embed = jnp.where(
        slot_live, jnp.take_along_axis(d_positions, inverse[:, :, None], axis=1), 0.0
    )
    d_embed_low = d_embed.reshape(images * slot_count, dec_width).astype(jnp.bfloat16)
    grad_embed = matmul_tn(enc_low, d_embed_low)
    d_enc = matmul_nt(d_embed_low, dec_again[0])
    dec_shares = (
        lax.psum_scatter(
            grad_embed.astype(jnp.bfloat16), "fsdp", scatter_dimension=0, tiled=True
        ).astype(jnp.float32),
        lax.psum_scatter(
            grad_mask.astype(jnp.bfloat16), "fsdp", scatter_dimension=0, tiled=True
        ).astype(jnp.float32),
        lax.psum_scatter(
            dec_grads[0].astype(jnp.bfloat16), "fsdp", scatter_dimension=0, tiled=True
        ).astype(jnp.float32),
        lax.psum_scatter(
            dec_grads[1].astype(jnp.bfloat16), "fsdp", scatter_dimension=0, tiled=True
        ).astype(jnp.float32),
        lax.psum_scatter(
            dec_grads[2].astype(jnp.bfloat16), "fsdp", scatter_dimension=0, tiled=True
        ).astype(jnp.float32),
        lax.psum_scatter(
            dec_grads[3].astype(jnp.bfloat16), "fsdp", scatter_dimension=0, tiled=True
        ).astype(jnp.float32),
        lax.psum_scatter(
            dec_grads[4].astype(jnp.bfloat16), "fsdp", scatter_dimension=0, tiled=True
        ).astype(jnp.float32),
        lax.psum_scatter(
            dec_grads[5].astype(jnp.bfloat16), "fsdp", scatter_dimension=0, tiled=True
        ).astype(jnp.float32),
    )
    dec_sums = (
        lax.psum(dec_shares[0].astype(jnp.bfloat16), "rep").astype(jnp.float32),
        lax.psum(dec_shares[1].astype(jnp.bfloat16), "rep").astype(jnp.float32),
        lax.psum(dec_shares[2].astype(jnp.bfloat16), "rep").astype(jnp.float32),
        lax.psum(dec_shares[3].astype(jnp.bfloat16), "rep").astype(jnp.float32),
        lax.psum(dec_shares[4].astype(jnp.bfloat16), "rep").astype(jnp.float32),
        lax.psum(dec_shares[5].astype(jnp.bfloat16), "rep").astype(jnp.float32),
        lax.psum(dec_shares[6].astype(jnp.bfloat16), "rep").astype(jnp.float32),
        lax.psum(dec_shares[7].astype(jnp.bfloat16), "rep").astype(jnp.float32),
    )
    enc_again = (
        lax.all_gather(enc_gain1, "fsdp", axis=0, tiled=True),
        lax.all_gather(enc_qkv, "fsdp", axis=0, tiled=True),
        lax.all_gather(enc_proj, "fsdp", axis=0, tiled=True),
        lax.all_gather(enc_gain2, "fsdp", axis=0, tiled=True),
        lax.all_gather(enc_up, "fsdp", axis=0, tiled=True),
        lax.all_gather(enc_down, "fsdp", axis=0, tiled=True),
    )
    d_rows_in, enc_grads = block_backward(
        enc_state, d_enc, enc_again, visible, HEADS, images, slot_count
    )
    enc_shares = (
        lax.psum_scatter(
            enc_grads[0].astype(jnp.bfloat16), "fsdp", scatter_dimension=0, tiled=True
        ).astype(jnp.float32),
        lax.psum_scatter(
            enc_grads[1].astype(jnp.bfloat16), "fsdp", scatter_dimension=0, tiled=True
        ).astype(jnp.float32),
        lax.psum_scatter(
            enc_grads[2].astype(jnp.bfloat16), "fsdp", scatter_dimension=0, tiled=True
        ).astype(jnp.float32),
        lax.psum_scatter(
            enc_grads[3].astype(jnp.bfloat16), "fsdp", scatter_dimension=0, tiled=True
        ).astype(jnp.float32),
        lax.psum_scatter(
            enc_grads[4].astype(jnp.bfloat16), "fsdp", scatter_dimension=0, tiled=True
        ).astype(jnp.float32),
        lax.psum_scatter(
            enc_grads[5].astype(jnp.bfloat16), "fsdp", scatter_dimension=0, tiled=True
        ).astype(jnp.float32),
    )
    enc_sums = (
        lax.psum(enc_shares[0].astype(jnp.bfloat16), "rep").astype(jnp.float32),
        lax.psum(enc_shares[1].astype(jnp.bfloat16), "rep").astype(jnp.float32),
        lax.psum(enc_shares[2].astype(jnp.bfloat16), "rep").astype(jnp.float32),
        lax.psum(enc_shares[3].astype(jnp.bfloat16), "rep").astype(jnp.float32),
        lax.psum(enc_shares[4].astype(jnp.bfloat16), "rep").astype(jnp.float32),
        lax.psum(enc_shares[5].astype(jnp.bfloat16), "rep").astype(jnp.float32),
    )
    return (
        enc_low.reshape(images, slot_count, model_width),
        dec_rows.astype(jnp.bfloat16).reshape(images, patch_count, dec_width),
        d_rows_in.astype(jnp.bfloat16).reshape(images, slot_count, model_width),
        enc_sums[0],
        enc_sums[1],
        enc_sums[2],
        enc_sums[3],
        enc_sums[4],
        enc_sums[5],
        dec_sums[0],
        dec_sums[1],
        dec_sums[2],
        dec_sums[3],
        dec_sums[4],
        dec_sums[5],
        dec_sums[6],
        dec_sums[7],
    )


def solution(mesh):
    placed = (
        P(("rep", "fsdp"), None, None),
        P("fsdp"),
        P("fsdp", None),
        P("fsdp", None),
        P("fsdp"),
        P("fsdp", None),
        P("fsdp", None),
        P("fsdp", None),
        P("fsdp"),
        P("fsdp"),
        P("fsdp", None),
        P("fsdp", None),
        P("fsdp"),
        P("fsdp", None),
        P("fsdp", None),
        P(("rep", "fsdp")),
        P(("rep", "fsdp"), None),
        P(("rep", "fsdp")),
        P(("rep", "fsdp"), None, None),
    )
    return jax.shard_map(
        shards,
        mesh=mesh,
        in_specs=placed,
        out_specs=(
            P(("rep", "fsdp"), None, None),
            P(("rep", "fsdp"), None, None),
            P(("rep", "fsdp"), None, None),
            P("fsdp"),
            P("fsdp", None),
            P("fsdp", None),
            P("fsdp"),
            P("fsdp", None),
            P("fsdp", None),
            P("fsdp", None),
            P("fsdp"),
            P("fsdp"),
            P("fsdp", None),
            P("fsdp", None),
            P("fsdp"),
            P("fsdp", None),
            P("fsdp", None),
        ),
        check_vma=False,
    )
```

profile of v0, /device:TPU:24, one launch (start us, length us, event | category | flops | bytes accessed | tf_op | source)
XLA Modules:
  0.0 1003.6 jit_solution(6294940363911702248)
XLA Ops:
  21.3 13.5 %all-reduce.9 = (bf16[512]{0:T(512)(128)(2,1)S(1)}, bf16[512]{0:T(512)(128)(2,1)S(1)}, bf16[512]{0:T(512)(128)(2,1)S(1)}) all-reduce(bf16[512]{0:T(512)(128)(2,1)S(1)} %dynamic-update-slice, bf16[512]{0:T(512)(128)(2,1)S(1)} %dynamic-update-slice.1, bf16[512]{0:T(512)(128)(2,1)S(1)} %dynamic-update-slice.2), channel_id=1, replica_groups=mesh['rep'=4,'fsdp'=8] {'fsdp'}, use_global_device_ids=true, to_apply=%add | all-reduce | flops 1536 | bytes 6144
  36.7 11.6 %all-gather = bf16[8,1,128]{2,1,0:T(2,128)(2,1)S(1)} all-gather(bf16[1,1,128]{2,1,0:T(2,128)(2,1)S(1)} %bitcast.330), channel_id=1, replica_groups=mesh['rep'=4,'fsdp'=8] {'fsdp'}, dimensions={0}, use_global_device_ids=true | all-gather | bytes 2304 | tf_op jit(solution)/shard_map/all_gather | solution.py:211
  57.0 19.3 %all_gather.65 = bf16[512,512]{1,0:T(8,128)(2,1)} all-gather(bf16[64,512]{1,0:T(8,128)(2,1)S(1)} %copy-done.46), channel_id=1, replica_groups=mesh['rep'=4,'fsdp'=8] {'fsdp'}, dimensions={0}, use_global_device_ids=true | all-gather | bytes 589824 | tf_op jit(solution)/shard_map/all_gather | solution.py:225
  130.1 60.1 %all-gather.15.cloned.1.call-done = bf16[1024,4096]{1,0:T(8,128)(2,1)} async-done(((bf16[128,4096]{1,0:T(8,128)(2,1)}), bf16[1024,4096]{1,0:T(8,128)(2,1)}) %all-gather.15.cloned.1.call-update) | async-done | bytes 8388624 | tf_op jit(solution)/shard_map/all_gather | solution.py:215
  190.2 27.5 %multiply_convert_fusion.2 = (bf16[512,4096]{1,0:T(8,128)(2,1)}, f32[512,4096]{1,0:T(8,128)}, f32[512,4096]{1,0:T(8,128)}) fusion(bf16[1024,4096]{1,0:T(8,128)(2,1)} %all-gather.15.cloned.1.call-done, f32[512,1024]{1,0:T(8,128)S(1)} %get-tuple-element.239, f32[1024]{0:T(1024)S(1)} %bitcast.318, f32[512]{0:T(512)S(1)} %add_rsqrt_fusion.2, ...), kind=kOutput, calls=%fused_computation.65 | convolution fusion | flops 4433379328 | bytes 31465472 | tf_op jit(solution)/shard_map/dot_general | solution.py:17
  217.8 54.5 %all-gather.17.cloned.1.call-done = bf16[4096,1024]{1,0:T(8,128)(2,1)} async-done(((bf16[512,1024]{1,0:T(8,128)(2,1)}), bf16[4096,1024]{1,0:T(8,128)(2,1)}) %all-gather.17.cloned.1.call-update) | async-done | bytes 8388624 | tf_op jit(solution)/shard_map/all_gather | solution.py:216
  272.3 10.1 %add_convert_fusion.3 = bf16[512,1024]{1,0:T(8,128)(2,1)} fusion(f32[512,1024]{1,0:T(8,128)S(1)} %get-tuple-element.239, bf16[512,4096]{1,0:T(8,128)(2,1)} %get-tuple-element.195, bf16[4096,1024]{1,0:T(8,128)(2,1)} %all-gather.17.cloned.1.call-done), kind=kOutput, calls=%fused_computation.146 | convolution fusion | flops 4296015872 | bytes 15728640 | tf_op jit(solution)/shard_map/dot_general | solution.py:17
  282.4 13.6 %all-gather.19.cloned.1.call-done = bf16[1024,512]{1,0:T(8,128)(2,1)} async-done(((bf16[128,512]{1,0:T(8,128)(2,1)}), bf16[1024,512]{1,0:T(8,128)(2,1)}) %all-gather.19.cloned.1.call-update) | async-done | bytes 1048592 | tf_op jit(solution)/shard_map/all_gather | solution.py:221
  331.7 18.1 %while.4 = (s32[]{:T(128)}, bf16[2,2,256,512]{3,2,1,0:T(8,128)(2,1)}, f32[2,2,16,256]{3,2,1,0:T(8,128)S(1)}, bf16[2,2,256,1536]{2,3,1,0:T(8,128)(2,1)}, s32[]{:T(128)}) while((s32[]{:T(128)}, bf16[2,2,256,512]{3,2,1,0:T(8,128)(2,1)}, f32[2,2,16,256]{3,2,1,0:T(8,128)S(1)}, bf16[2,2,256,1536]{2,3,1,0:T(8,128)(2,1)}, s32[]{:T(128)}) %tuple.97), condition=%wide.region_11.12_spmd, body=%wide.region_8.11_spmd.sunk | while | flops 293855744 | bytes 32771152 | solution.py:65
  353.8 24.3 %multiply_convert_fusion.1 = (bf16[1024,2048]{1,0:T(8,128)(2,1)}, f32[1024,2048]{1,0:T(8,128)}, f32[1024,2048]{1,0:T(8,128)}) fusion(bf16[512,2048]{1,0:T(8,128)(2,1)} %all-gather.23.cloned.1.call-done, f32[1024,512]{1,0:T(8,128)} %copy-done.14, f32[512]{0:T(512)S(1)} %copy-done.73, f32[1024]{0:T(1024)S(1)} %add_rsqrt_fusion, ...), kind=kOutput, calls=%fused_computation.52 | convolution fusion | flops 2285895680 | bytes 25176064 | tf_op jit(solution)/shard_map/dot_general | solution.py:17
  381.9 8.8 add_convert_fusion.1
  400.7 32.4 %while.5 = (s32[]{:T(128)}, bf16[2,2,256,1536]{3,2,1,0:T(8,128)(2,1)}, bf16[2,2,256,1536]{2,3,1,0:T(8,128)(2,1)}, f32[2,2,16,256]{3,2,1,0:T(8,128)S(1)}, bf16[2,2,256,512]{3,2,1,0:T(8,128)(2,1)}, /*index=5*/s32[]{:T(128)}) while((s32[]{:T(128)}, bf16[2,2,256,1536]{3,2,1,0:T(8,128)(2,1)}, bf16[2,2,256,1536]{2,3,1,0:T(8,128)(2,1)}, ...), condition=%wide.region_19.20_spmd, body=%wide.region_17.19_spmd.sunk | while | flops 705421824 | bytes 86215256 | solution.py:65
  469.6 15.3 %add_convert_fusion = bf16[512,4096]{1,0:T(8,128)(2,1)} fusion(f32[512,4096]{1,0:T(8,128)} %get-tuple-element.196, f32[512,4096]{1,0:T(8,128)} %get-tuple-element.240, bf16[4096,1024]{1,0:T(8,128)(2,1)} %all-gather.17.cloned.1.call-done, f32[512,1024]{1,0:T(8,128)S(1)} %fusion.105), kind=kOutput, calls=%fused_computation.50 | convolution fusion | flops 4324851712 | bytes 31457280 | tf_op jit(solution)/shard_map/dot_general | solution.py:27
  532.6 9.3 convolution_convert_fusion.1
  543.5 9.0 convolution_convert_fusion
  552.7 35.0 %reduce-scatter.24.cloned.1.call-done = bf16[64,2048]{1,0:T(8,128)(2,1)} async-done(((bf16[512,2048]{1,0:T(8,128)(2,1)}), bf16[64,2048]{1,0:T(8,128)(2,1)}) %reduce-scatter.24.cloned.1.call-update) | async-done | bytes 262160 | tf_op jit(solution)/shard_map/reduce_scatter | solution.py:291
  587.8 36.8 %reduce-scatter.12.cloned.1.call-done = bf16[128,1024]{1,0:T(8,128)(2,1)} async-done(((bf16[1024,1024]{1,0:T(8,128)(2,1)}), bf16[128,1024]{1,0:T(8,128)(2,1)}) %reduce-scatter.12.cloned.1.call-update) | async-done | bytes 262160 | tf_op jit(solution)/shard_map/reduce_scatter | solution.py:326
  624.5 71.8 %reduce-scatter.10.cloned.1.call-done = bf16[128,3072]{1,0:T(8,128)(2,1)} async-done(((bf16[1024,3072]{1,0:T(8,128)(2,1)}), bf16[128,3072]{1,0:T(8,128)(2,1)}) %reduce-scatter.10.cloned.1.call-update) | async-done | bytes 786448 | tf_op jit(solution)/shard_map/reduce_scatter | solution.py:323
  696.3 90.3 %reduce-scatter.14.cloned.1.call-done = bf16[128,4096]{1,0:T(8,128)(2,1)} async-done(((bf16[1024,4096]{1,0:T(8,128)(2,1)}), bf16[128,4096]{1,0:T(8,128)(2,1)}) %reduce-scatter.14.cloned.1.call-update) | async-done | bytes 1048592 | tf_op jit(solution)/shard_map/reduce_scatter | solution.py:332
  786.6 90.3 %reduce-scatter.16.cloned.1.call-done = bf16[512,1024]{1,0:T(8,128)(2,1)} async-done(((bf16[4096,1024]{1,0:T(8,128)(2,1)}), bf16[512,1024]{1,0:T(8,128)(2,1)}) %reduce-scatter.16.cloned.1.call-update) | async-done | bytes 1048592 | tf_op jit(solution)/shard_map/reduce_scatter | solution.py:335
  878.2 9.0 fusion.62
  887.2 12.9 %all-reduce.8 = (bf16[1024]{0:T(1024)(128)(2,1)S(1)}, bf16[1024]{0:T(1024)(128)(2,1)S(1)}, bf16[512]{0:T(512)(128)(2,1)S(1)}, bf16[512]{0:T(512)(128)(2,1)S(1)}, bf16[512]{0:T(512)(128)(2,1)S(1)}) all-reduce(bf16[1024]{0:T(1024)(128)(2,1)S(1)} %get-tuple-element.143, ...), channel_id=2, replica_groups=mesh['rep'=4,'fsdp'=8] {'fsdp'}, use_global_device_ids=true, to_apply=%region_28.29.clone | all-reduce | flops 3584 | bytes 14336
  900.5 9.8 all-reduce.10
  922.9 57.0 %all-reduce.14.cloned.1.call-done = (bf16[128,3072]{1,0:T(8,128)(2,1)}, bf16[128,1024]{1,0:T(8,128)(2,1)}, bf16[128,4096]{1,0:T(8,128)(2,1)}, bf16[512,1024]{1,0...) async-done(((bf16[128,3072]{1,0:T(8,128)(2,1)}, ...) | async-done | bytes 4063248 | tf_op jit(solution)/shard_map/psum | solution.py:341
  (384 shorter events, 293.9 us)
Async XLA Ops:
  8.8 81.0 %all-gather.11.cloned.1.call-start = ((), (), s32[]{:S(2)}) async-start(), calls=%async_computation.9 | async-start | bytes 7077888 | tf_op jit(solution)/shard_map/all_gather | solution.py:212
  9.4 117.0 %all-gather.13.cloned.1.call-start = ((), (), s32[]{:S(2)}) async-start(), calls=%async_computation.10 | async-start | bytes 2359296 | tf_op jit(solution)/shard_map/all_gather | solution.py:213
  10.0 180.3 %all-gather.15.cloned.1.call-start = ((), (), s32[]{:S(2)}) async-start(), calls=%async_computation.11 | async-start | bytes 9437184 | tf_op jit(solution)/shard_map/all_gather | solution.py:215
  10.6 261.7 %all-gather.17.cloned.1.call-start = ((), (), s32[]{:S(2)}) async-start(), calls=%async_computation.12 | async-start | bytes 9437184 | tf_op jit(solution)/shard_map/all_gather | solution.py:216
  11.3 284.7 %all-gather.19.cloned.1.call-start = ((), (), s32[]{:S(2)}) async-start(), calls=%async_computation.13 | async-start | bytes 1179648 | tf_op jit(solution)/shard_map/all_gather | solution.py:221
  12.0 310.0 %all-gather.21.cloned.1.call-start = ((), (), s32[]{:S(2)}) async-start(), calls=%async_computation.14 | async-start | bytes 1769472 | tf_op jit(solution)/shard_map/all_gather | solution.py:224
  12.8 341.0 %all-gather.23.cloned.1.call-start = ((), (), s32[]{:S(2)}) async-start(), calls=%async_computation.15 | async-start | bytes 2359296 | tf_op jit(solution)/shard_map/all_gather | solution.py:227
  13.4 368.5 %all-gather.25.cloned.1.call-start = ((), (), s32[]{:S(2)}) async-start(), calls=%async_computation.16 | async-start | bytes 2359296 | tf_op jit(solution)/shard_map/all_gather | solution.py:228
  14.0 538.7 %reduce-scatter.22.cloned.1.call-start = ((), (), s32[]{:S(2)}) async-start(), calls=%async_computation.23 | async-start | bytes 589824 | tf_op jit(solution)/shard_map/reduce_scatter | solution.py:285
  34.8 287.3 %copy-start.59 = (f32[512]{0:T(512)}, f32[512]{0:T(512)S(1)}, u32[]{:S(2)}) copy-start(f32[512]{0:T(512)S(1)} %convert_element_type.322) | copy-start | bytes 6148
  36.6 274.3 %copy-start.68 = (pred[1024]{0:T(1024)(128)(4,1)}, pred[1024]{0:T(1024)(128)(4,1)S(1)}, u32[]{:S(2)}) copy-start(pred[1024]{0:T(1024)(128)(4,1)S(1)} %broadcast_in_dim.215) | copy-start | bytes 3076
  56.8 133.4 %copy-start.62 = (f32[8,1,128]{2,1,0:T(1,128)}, f32[8,1,128]{2,1,0:T(1,128)S(1)}, u32[]{:S(2)}) copy-start(f32[8,1,128]{2,1,0:T(1,128)S(1)} %convert_element_type.375) | copy-start | bytes 12292
  129.7 142.6 %copy-start.7 = (f32[512,1024]{1,0:T(8,128)}, f32[512,1024]{1,0:T(8,128)S(1)}, u32[]{:S(2)}) copy-start(f32[512,1024]{1,0:T(8,128)S(1)} %get-tuple-element.239) | copy-start | bytes 6291460
  400.6 152.1 %reduce-scatter.18.cloned.1.call-start = ((), (), s32[]{:S(2)}) async-start(), calls=%async_computation.21 | async-start | bytes 1179648 | tf_op jit(solution)/shard_map/reduce_scatter | solution.py:273
  449.4 103.3 %reduce-scatter.20.cloned.1.call-start = ((), (), s32[]{:S(2)}) async-start(), calls=%async_computation.22 | async-start | bytes 1769472 | tf_op jit(solution)/shard_map/reduce_scatter | solution.py:282
  455.0 97.7 %reduce-scatter.26.cloned.1.call-start = ((), (), s32[]{:S(2)}) async-start(), calls=%async_computation.25 | async-start | bytes 2359296 | tf_op jit(solution)/shard_map/reduce_scatter | solution.py:294
  461.3 126.5 %reduce-scatter.24.cloned.1.call-start = ((), (), s32[]{:S(2)}) async-start(), calls=%async_computation.24 | async-start | bytes 2359296 | tf_op jit(solution)/shard_map/reduce_scatter | solution.py:291
  467.5 157.0 %reduce-scatter.12.cloned.1.call-start = ((), (), s32[]{:S(2)}) async-start(), calls=%async_computation.18 | async-start | bytes 2359296 | tf_op jit(solution)/shard_map/reduce_scatter | solution.py:326
  498.4 197.9 %reduce-scatter.10.cloned.1.call-start = ((), (), s32[]{:S(2)}) async-start(), calls=%async_computation.17 | async-start | bytes 7077888 | tf_op jit(solution)/shard_map/reduce_scatter | solution.py:323
  532.6 254.0 %reduce-scatter.14.cloned.1.call-start = ((), (), s32[]{:S(2)}) async-start(), calls=%async_computation.19 | async-start | bytes 9437184 | tf_op jit(solution)/shard_map/reduce_scatter | solution.py:332
  541.9 334.9 %reduce-scatter.16.cloned.1.call-start = ((), (), s32[]{:S(2)}) async-start(), calls=%async_computation.20 | async-start | bytes 9437184 | tf_op jit(solution)/shard_map/reduce_scatter | solution.py:335
  552.5 325.6 %copy-start.52 = (f32[512]{0:T(512)S(1)}, f32[512]{0:T(512)}, u32[]{:S(2)}) copy-start(f32[512]{0:T(512)} %copy-done.51) | copy-start | bytes 6148
  552.5 325.6 %copy-start.54 = (f32[512]{0:T(512)S(1)}, f32[512]{0:T(512)}, u32[]{:S(2)}) copy-start(f32[512]{0:T(512)} %copy-done.53) | copy-start | bytes 6148
  552.6 427.3 %all-reduce.14.cloned.1.call-start = ((), (), s32[]{:S(2)}) async-start(), calls=%async_computation.26 | async-start | bytes 8126464 | tf_op jit(solution)/shard_map/psum | solution.py:341
  (78 other events, 1193.4 us)
Sparse Core Ops, SparseCore 0:
  11.8 2.5 sort.21.cloned.1.call-done
  877.0 102.8 all-reduce.13
  (1 shorter events, 0.0 us)
Sparse Core Ops, SparseCore 1:
  10.9 67.4 all-gather.10
  79.9 28.7 all-gather.12
  110.1 80.0 all-gather.14
  191.9 80.4 all-gather.16
  273.9 22.1 all-gather.18
  297.7 24.3 all-gather.20
  323.5 28.4 all-gather.22
  353.5 28.4 all-gather.24
  400.7 28.7 reduce-scatter.21
  449.5 29.7 reduce-scatter.17
  482.0 32.2 reduce-scatter.19
  516.6 34.4 reduce-scatter.25
  553.2 34.5 reduce-scatter.23
  590.1 34.4 reduce-scatter.11
  626.8 69.4 reduce-scatter.9
  698.6 87.9 reduce-scatter.13
  788.9 87.9 reduce-scatter.15
where the time goes:
time: 1010 us; the launch traced here: 1000 us
  waiting for transfers between devices  527 us (52%)
  matrix products  230 us (23%)
  local copies, waits for them, and re-layouts  84.7 us (8%)
  blocking collectives  75.6 us (7%)
  other arithmetic  64.8 us (6%)
  between operations  19.3 us (2%)
    reduce_scatter x1, waiting for transfers between devices, shards(): lax.psum_scatter(enc_grads[5].astype(jnp.bfloat16), 'fsdp', scatter_dimen...  90.3 us
    reduce_scatter x1, waiting for transfers between devices, shards(): lax.psum_scatter(enc_grads[4].astype(jnp.bfloat16), 'fsdp', scatter_dimen...  90.3 us
    dot_general x9, matrix products, matmul(): return jnp.dot(left, right, preferred_element_type=jnp.float32)  87.6 us
    reduce_scatter x1, waiting for transfers between devices, shards(): lax.psum_scatter(enc_grads[1].astype(jnp.bfloat16), 'fsdp', scatter_dimen...  71.8 us
    all_gather x1, waiting for transfers between devices, shards(): lax.all_gather(enc_up, 'fsdp', axis=0, tiled=True)  60.1 us
    dot_general x9, matrix products, matmul_nt(): lax.dot_general(left, right, (((1,), (1,)), ((), ())), preferred_element_...  58.9 us
    psum x1, waiting for transfers between devices, shards(): lax.psum(enc_shares[1].astype(jnp.bfloat16), 'rep').astype(jnp.float32)  57 us
    all_gather x1, waiting for transfers between devices, shards(): lax.all_gather(enc_down, 'fsdp', axis=0, tiled=True)  54.5 us
  transfers between devices with their start and end apart: 18, of which 11 were waited for; matrix products, arithmetic and copies ran while one was open for 34% of the time, Pallas kernels for 0%

commit v1 on v0

--- a/solution.py
+++ b/solution.py
@@ -1,8 +1,11 @@
+import functools
 import math
 
 import jax
 import jax.numpy as jnp
 from jax import lax
+from jax.experimental import pallas as pl
+from jax.experimental.pallas import tpu as pltpu
 from jax.sharding import PartitionSpec as P
 
 HEADS = 16
@@ -183,7 +186,498 @@
     return (d_rows, (grad_gain_one, grad_qkv, grad_out, grad_gain_two, grad_up, grad_down))
 
 
+MESH_ID = pl.DeviceIdType.MESH
+
+
+def places():
+    rep = lax.axis_index("rep")
+    own = lax.axis_index("fsdp")
+    return rep, own, own // 2, own % 2
+
+
+def dev(rep, own):
+    return {"rep": rep, "fsdp": own}
+
+
+def greet(rep, own, line, length):
+    barrier = pltpu.get_barrier_semaphore()
+
+    def call(r, f):
+        pl.semaphore_signal(barrier, inc=1, device_id=dev(r, f), device_id_type=MESH_ID)
+
+    call(rep, own + 1 - 2 * (own % 2))
+    call(rep + 1 - 2 * (rep % 2), own)
+    call((rep + 2) % 4, own)
+
+    @pl.when(line > 0)
+    def _():
+        call(rep, own - 2)
+
+    @pl.when(line < length - 1)
+    def _():
+        call(rep, own + 2)
+
+    ends = (line == 0).astype(jnp.int32) + (line == length - 1).astype(jnp.int32)
+    pl.semaphore_wait(barrier, 5 - ends)
+
+
+def gather_kernel(shapes, length, *refs):
+    count = len(shapes)
+    ins, outs, rest = (refs[:count], refs[count : 2 * count], refs[2 * count :])
+    (own_sem, q_send, q_recv, o_send, z_send, z_recv, x_send, x_recv, y_send, y_recv) = rest[:10]
+    d_send, d_recv, p_send, p_recv = rest[10:]
+    rep, own, line, core = places()
+    x_peer, y_peer = (rep + 1 - 2 * (rep % 2), (rep + 2) % 4)
+    mate = own + 1 - 2 * core
+    greet(rep, own, line, length)
+
+    def window(k, source, quarter):
+        rows, cols = shapes[k]
+        start = pl.multiple_of((2 * source + core) * rows, 16)
+        if quarter is None:
+            return outs[k].at[pl.ds(start, rows), :]
+        return outs[k].at[
+            pl.ds(start, rows), pl.ds(pl.multiple_of(quarter * (cols // 4), 128), cols // 4)
+        ]
+
+    def send(src, dst, s_sem, r_sem, r, f):
+        return pltpu.make_async_remote_copy(
+            src_ref=src, dst_ref=dst, send_sem=s_sem, recv_sem=r_sem,
+            device_id=dev(r, f), device_id_type=MESH_ID,
+        )
+
+    def mine(k):
+        _, cols = shapes[k]
+        return ins[k].at[:, pl.ds(pl.multiple_of(rep * (cols // 4), 128), cols // 4)]
+
+    def left(k):
+        return send(mine(k), window(k, line, rep), o_send.at[k, 0], z_recv.at[k, line], rep, own - 2)
+
+    def right(k):
+        return send(mine(k), window(k, line, rep), o_send.at[k, 1], z_recv.at[k, line], rep, own + 2)
+
+    def start_own(k):
+        @pl.when(line > 0)
+        def _():
+            left(k).start()
+
+        @pl.when(line < length - 1)
+        def _():
+            right(k).start()
+
+    def local(k):
+        rows, _ = shapes[k]
+        return pltpu.make_async_copy(
+            ins[k], outs[k].at[pl.ds(pl.multiple_of(own * rows, 16), rows), :], own_sem.at[k]
+        )
+
+    def to_mate(k):
+        rows, _ = shapes[k]
+        return send(
+            ins[k], outs[k].at[pl.ds(pl.multiple_of(own * rows, 16), rows), :],
+            q_send.at[k], q_recv.at[k], rep, mate,
+        )
+
+    def z_step(k, s, sign):
+        w = window(k, s, rep)
+        return send(w, w, z_send.at[k, s], z_recv.at[k, s], rep, own - 2 * sign)
+
+    def x_step(k, s):
+        w = window(k, s, rep)
+        return send(w, w, x_send.at[k, s], x_recv.at[k, s], x_peer, own)
+
+    def y_step(k, s):
+        w = window(k, s, rep)
+        return send(w, w, y_send.at[k, s], y_recv.at[k, s], y_peer, own)
+
+    def d_by_y(k, s):
+        w = window(k, s, x_peer)
+        return send(w, w, d_send.at[k, s], d_recv.at[k, s], y_peer, own)
+
+    def d_by_x(k, s):
+        w = window(k, s, y_peer)
+        return send(w, w, d_send.at[k, s], d_recv.at[k, s], x_peer, own)
+
+    def p_step(k, s):
+        w = window(k, s, None)
+        return send(w, w, p_send.at[k, s], p_recv.at[k, s], rep, mate)
+
+    items = [(k, h, sign) for k in range(count) for h in range(1, length) for sign in (1, -1)]
+
+    def each(item, body):
+        k, h, sign = item
+        s = line + sign * h
+        if sign > 0:
+            there, further = s < length, line > 0
+        else:
+            there, further = s >= 0, line < length - 1
+
+        @pl.when(there)
+        def _():
+            body(k, s, sign, further)
+
+    def stage_z(k, s, sign, further):
+        z_step(k, s, sign).wait_recv()
+
+        @pl.when(further)
+        def _():
+            z_step(k, s, sign).start()
+
+        x_step(k, s).start()
+        y_step(k, s).start()
+
+    def stage_xy(k, s, sign, further):
+        x_step(k, s).wait_recv()
+        y_step(k, s).wait_recv()
+
+        @pl.when(s % 2 == 0)
+        def _():
+            d_by_y(k, s).start()
+
+        @pl.when(s % 2 == 1)
+        def _():
+            d_by_x(k, s).start()
+
+    def stage_d(k, s, sign, further):
+        d_by_x(k, s).wait_recv()
+        p_step(k, s).start()
+
+    def stage_end(k, s, sign, further):
+        @pl.when(further)
+        def _():
+            z_step(k, s, sign).wait_send()
+
+        x_step(k, s).wait_send()
+        y_step(k, s).wait_send()
+        d_by_x(k, s).wait_send()
+        p_step(k, s).wait_send()
+        p_step(k, s).wait_recv()
+
+    start_own(0)
+    if count > 1:
+        start_own(1)
+    for k in range(count):
+        local(k).start()
+        to_mate(k).start()
+    lag, total = 2, len(items)
+    for i in range(total + 2 * lag):
+        if i < total:
+            k, h, sign = items[i]
+            if h == 1 and sign == 1 and k >= 1 and k + 1 < count:
+                start_own(k + 1)
+            each(items[i], stage_z)
+        if 0 <= i - lag < total:
+            each(items[i - lag], stage_xy)
+        if 0 <= i - 2 * lag < total:
+            each(items[i - 2 * lag], stage_d)
+    for item in items:
+        each(item, stage_end)
+    for k in range(count):
+        local(k).wait()
+        to_mate(k).wait()
+
+        @pl.when(line > 0)
+        def _():
+            left(k).wait_send()
+
+        @pl.when(line < length - 1)
+        def _():
+            right(k).wait_send()
+
+
+def gather_all(shards, length, ident):
+    shapes = tuple(s.shape for s in shards)
+    count = len(shapes)
+    sem = pltpu.SemaphoreType.DMA
+    return pl.pallas_call(
+        functools.partial(gather_kernel, shapes, length),
+        out_shape=tuple(
+            jax.ShapeDtypeStruct((2 * length * rows, cols), jnp.bfloat16) for rows, cols in shapes
+        ),
+        in_specs=[pl.BlockSpec(memory_space=pltpu.VMEM)] * count,
+        out_specs=tuple(pl.BlockSpec(memory_space=pl.ANY) for _ in shapes),
+        scratch_shapes=[sem((count,)), sem((count,)), sem((count,)), sem((count, 2))]
+        + [sem((count, length))] * 10,
+        compiler_params=pltpu.CompilerParams(collective_id=ident, has_side_effects=True),
+        name="gather_all",
+    )(*shards)
+
+
+def reduce_kernel(shapes, length, *refs):
+    count = len(shapes)
+    ins, outs, rest = (refs[:count], refs[count : 2 * count], refs[2 * count :])
+    held, other, first, second, third, fourth = (
+        rest[count * j : count * (j + 1)] for j in range(6)
+    )
+    rest = rest[6 * count :]
+    (l_sem, p_send, p_recv, a_send, a_recv, b_send, b_recv, z_send, z_recv) = rest[:9]
+    (w_recv, e_sem, f_send, f_recv, g_send, g_recv, h_send, h_recv) = rest[9:]
+    rep, own, line, core = places()
+    x_bit, y_bit = rep % 2, rep // 2
+    x_peer, y_peer = (rep + 1 - 2 * x_bit, (rep + 2) % 4)
+    mate = own + 1 - 2 * core
+    greet(rep, own, line, length)
+
+    def send(src, dst, s_sem, r_sem, r, f):
+        return pltpu.make_async_remote_copy(
+            src_ref=src, dst_ref=dst, send_sem=s_sem, recv_sem=r_sem,
+            device_id=dev(r, f), device_id_type=MESH_ID,
+        )
+
+    def bits(t):
+        if t % 2 == 0:
+            return x_bit, y_bit, x_peer, y_peer
+        return y_bit, x_bit, y_peer, x_peer
+
+    def block(k, t, side):
+        rows, _ = shapes[k]
+        return ins[k].at[pl.ds(pl.multiple_of((2 * t + side) * rows, 16), rows), :]
+
+    def load(k, t):
+        return pltpu.make_async_copy(block(k, t, core), held[k].at[t], l_sem.at[k, t])
+
+    def p_step(k, t):
+        return send(
+            block(k, t, 1 - core), other[k].at[t], p_send.at[k, t], p_recv.at[k, t], rep, mate
+        )
+
+    def cut(index, width):
+        return pl.ds(pl.multiple_of(index * width, 128), width)
+
+    def a_step(k, t):
+        a, _, peer, _ = bits(t)
+        half = shapes[k][1] // 2
+        return send(
+            held[k].at[t, :, cut(1 - a, half)], first[k].at[t],
+            a_send.at[k, t], a_recv.at[k, t], peer, own,
+        )
+
+    def b_step(k, t):
+        _, b, _, peer = bits(t)
+        quarter = shapes[k][1] // 4
+        return send(
+            first[k].at[t, :, cut(1 - b, quarter)], second[k].at[t],
+            b_send.at[k, t], b_recv.at[k, t], peer, own,
+        )
+
+    def z_right(k, t):
+        if t == length:
+            return None
+        return send(second[k].at[t], third[k].at[t], z_send.at[k, t], z_recv.at[k, t], rep, own + 2)
+
+    def z_left(k, t, last):
+        dst, sem = (fourth[k], w_recv.at[k]) if last else (third[k].at[t], z_recv.at[k, t])
+        return send(second[k].at[t], dst, z_send.at[k, t], sem, rep, own - 2)
+
+    def add(k, rows, body):
+        step = 16 if rows % 32 else 32
+
+        @pl.loop(0, rows, step=step)
+        def _(r):
+            body(pl.ds(pl.multiple_of(r, 16), step))
+
+    def stage_a(k, t):
+        load(k, t).wait()
+        p_step(k, t).wait_recv()
+
+        def body(r):
+            held[k][t, r, :] = held[k][t, r, :] + other[k][t, r, :]
+
+        add(k, shapes[k][0], body)
+        a_step(k, t).start()
+
+    def stage_b(k, t):
+        a, _, _, _ = bits(t)
+        half = shapes[k][1] // 2
+        a_step(k, t).wait_recv()
+
+        def body(r):
+            first[k][t, r, :] = first[k][t, r, :] + held[k][t, r, cut(a, half)]
+
+        add(k, shapes[k][0], body)
+        b_step(k, t).start()
+
+    def stage_c(k, t):
+        _, b, _, _ = bits(t)
+        quarter = shapes[k][1] // 4
+        b_step(k, t).wait_recv()
+
+        def body(r):
+            second[k][t, r, :] = second[k][t, r, :] + first[k][t, r, cut(b, quarter)]
+
+        add(k, shapes[k][0], body)
+
+    def join(k, t, source):
+        def body(r):
+            second[k][t, r, :] = second[k][t, r, :] + source[r, :]
+
+        add(k, shapes[k][0], body)
+
+    def stage_z(k, t, hop):
+        if hop < t:
+
+            @pl.when(line == hop)
+            def _():
+                if hop > 0:
+                    z_right(k, t).wait_recv()
+                    join(k, t, third[k].at[t])
+                z_right(k, t).start()
+
+        place = length - 1 - hop
+        if place > t:
+
+            @pl.when(line == place)
+            def _():
+                if hop > 0:
+                    z_left(k, t, False).wait_recv()
+                    join(k, t, third[k].at[t])
+                z_left(k, t, place - 1 == t).start()
+
+    def piece(k, t, flip_a, flip_b):
+        a, b, _, _ = bits(t)
+        a = 1 - a if flip_a else a
+        b = 1 - b if flip_b else b
+        return outs[k].at[:, cut(2 * a + b, shapes[k][1] // 4)]
+
+    def put(k, t):
+        return pltpu.make_async_copy(second[k].at[t], piece(k, t, 0, 0), e_sem.at[k])
+
+    def f_step(k, t):
+        return send(
+            second[k].at[t], piece(k, t, 0, 0), f_send.at[k], f_recv.at[k], bits(t)[2], own
+        )
+
+    def g_step(k, t):
+        return send(
+            second[k].at[t], piece(k, t, 0, 0), g_send.at[k], g_recv.at[k], bits(t)[3], own
+        )
+
+    def h_first(k, t):
+        w = piece(k, t, 0, 1)
+        return send(w, w, h_send.at[k], h_recv.at[k], bits(t)[2], own)
+
+    def h_second(k, t):
+        w = piece(k, t, 1, 0)
+        return send(w, w, h_send.at[k], h_recv.at[k], bits(t)[3], own)
+
+    def stage_e(k, t):
+        @pl.when(line == t)
+        def _():
+            if t > 0:
+                z_right(k, t).wait_recv()
+                join(k, t, third[k].at[t])
+            if t < length - 1:
+                z_left(k, t, True).wait_recv()
+                join(k, t, fourth[k])
+            put(k, t).start()
+            f_step(k, t).start()
+            g_step(k, t).start()
+
+    def stage_f(k, t):
+        @pl.when(line == t)
+        def _():
+            f_step(k, t).wait_recv()
+            g_step(k, t).wait_recv()
+
+            @pl.when(core == 0)
+            def _():
+                h_first(k, t).start()
+
+            @pl.when(core == 1)
+            def _():
+                h_second(k, t).start()
+
+    items = [(k, t) for k in range(count) for t in range(length)]
+    for item in items:
+        load(*item).start()
+        p_step(*item).start()
+    total, lag = len(items), 2
+    plan = [(0, stage_a), (lag, stage_b), (2 * lag, stage_c)]
+    for hop in range(length - 1):
+        plan.append((3 * lag - 2 + hop * lag, functools.partial(stage_z, hop=hop)))
+    plan.append((3 * lag - 2 + (length - 1) * lag, stage_e))
+    plan.append((3 * lag - 2 + (length + 1) * lag, stage_f))
+    for i in range(total + plan[-1][0]):
+        for late, stage in plan:
+            if 0 <= i - late < total:
+                stage(*items[i - late])
+    for k, t in items:
+        p_step(k, t).wait_send()
+        a_step(k, t).wait_send()
+        b_step(k, t).wait_send()
+
+        @pl.when(line < t)
+        def _():
+            z_right(k, t).wait_send()
+
+        @pl.when(line > t)
+        def _():
+            z_left(k, t, False).wait_send()
+
+        @pl.when(line == t)
+        def _():
+            put(k, t).wait()
+            f_step(k, t).wait_send()
+            g_step(k, t).wait_send()
+            h_first(k, t).wait_send()
+            h_first(k, t).wait_recv()
+
+
+def reduce_all(arrays, length, ident):
+    shapes = tuple((a.shape[0] // (2 * length), a.shape[1]) for a in arrays)
+    count = len(shapes)
+    sem = pltpu.SemaphoreType.DMA
+
+    def room(part, lead=True):
+        return [
+            pltpu.VMEM(((length,) if lead else ()) + (rows, cols // part), jnp.bfloat16)
+            for rows, cols in shapes
+        ]
+
+    return pl.pallas_call(
+        functools.partial(reduce_kernel, shapes, length),
+        out_shape=tuple(jax.ShapeDtypeStruct(s, jnp.bfloat16) for s in shapes),
+        in_specs=[pl.BlockSpec(memory_space=pl.ANY)] * count,
+        out_specs=tuple(pl.BlockSpec(memory_space=pl.ANY) for _ in shapes),
+        scratch_shapes=room(1) + room(1) + room(2) + room(4) + room(4) + room(4, False)
+        + [sem((count, length))] * 9
+        + [sem((count,))] * 8,
+        compiler_params=pltpu.CompilerParams(
+            collective_id=ident, has_side_effects=True, vmem_limit_bytes=64 * 1024 * 1024 - 65536
+        ),
+        name="reduce_all",
+    )(*arrays)
+
+
+def vectors_in(vectors):
+    flat = jnp.concatenate(vectors)
+    wide = 512 * -(-flat.shape[0] // 512)
+    flat = jnp.pad(flat, (0, wide - flat.shape[0]))
+    return jnp.broadcast_to(flat[None, :], (16, wide))
+
+
+def vectors_out(packed, sizes):
+    table = packed.reshape(packed.shape[0] // 16, 16, packed.shape[1])[:, 0]
+    results, offset = [], 0
+    for size in sizes:
+        results.append(table[:, offset : offset + size].reshape(-1))
+        offset += size
+    return results
+
+
+def gather_plain(shards_of):
+    return [lax.all_gather(shard, "fsdp", axis=0, tiled=True) for shard in shards_of]
+
+
+def reduce_plain(arrays):
+    return [
+        lax.psum(lax.psum_scatter(array, "fsdp", scatter_dimension=0, tiled=True), "rep")
+        for array in arrays
+    ]
+
+
 def shards(
+    extents,
     patches,
     enc_gain1,
     enc_qkv,
@@ -207,57 +701,55 @@
     images, slot_count, model_width = patches.shape
     patch_count = unshuffle.shape[1]
     dec_width = embed_w.shape[1]
-    enc_full = (
-        lax.all_gather(enc_gain1, "fsdp", axis=0, tiled=True),
-        lax.all_gather(enc_qkv, "fsdp", axis=0, tiled=True),
-        lax.all_gather(enc_proj, "fsdp", axis=0, tiled=True),
-        lax.all_gather(enc_gain2, "fsdp", axis=0, tiled=True),
-        lax.all_gather(enc_up, "fsdp", axis=0, tiled=True),
-        lax.all_gather(enc_down, "fsdp", axis=0, tiled=True),
-    )
+    members = extents["fsdp"]
+    direct = members == 8 and extents["rep"] == 4
+
+    vectors = (enc_gain1, enc_gain2, mask_token, dec_gain1, dec_gain2)
+    sizes = [v.shape[0] for v in vectors]
+    weights = (
+        vectors_in(vectors),
+        enc_qkv,
+        enc_proj,
+        enc_up,
+        enc_down,
+        embed_w,
+        dec_qkv,
+        dec_proj,
+        dec_up,
+        dec_down,
+    )
+    if direct:
+        whole = gather_all(weights, members // 2, 0)
+    else:
+        whole = gather_plain(weights)
+    full_gain1, full_gain2, full_mask, full_dec1, full_dec2 = vectors_out(whole[0], sizes)
+    enc_full = (full_gain1, whole[1], whole[2], full_gain2, whole[3], whole[4])
+    dec_full = (full_dec1, whole[6], whole[7], full_dec2, whole[8], whole[9])
+    full_embed = whole[5]
+
     rows_in = patches.astype(jnp.float32).reshape(images * slot_count, model_width)
     enc_rows, enc_state = block_forward(rows_in, enc_full, visible, HEADS, images, slot_count)
-    dec_full = (
-        lax.all_gather(embed_w, "fsdp", axis=0, tiled=True),
-        lax.all_gather(mask_token, "fsdp", axis=0, tiled=True),
-        lax.all_gather(dec_gain1, "fsdp", axis=0, tiled=True),
-        lax.all_gather(dec_qkv, "fsdp", axis=0, tiled=True),
-        lax.all_gather(dec_proj, "fsdp", axis=0, tiled=True),
-        lax.all_gather(dec_gain2, "fsdp", axis=0, tiled=True),
-        lax.all_gather(dec_up, "fsdp", axis=0, tiled=True),
-        lax.all_gather(dec_down, "fsdp", axis=0, tiled=True),
-    )
     enc_low = enc_rows.astype(jnp.bfloat16)
-    embedded = matmul(enc_low, dec_full[0]).reshape(images, slot_count, dec_width)
+    embedded = matmul(enc_low, full_embed).reshape(images, slot_count, dec_width)
     picked = jnp.take_along_axis(
         embedded, jnp.minimum(unshuffle, slot_count - 1)[:, :, None], axis=1
     )
     shown_rows = (unshuffle < visible[:, None])[:, :, None]
     dec_in = jnp.where(
-        shown_rows, picked, dec_full[1].astype(jnp.float32)[None, None, :]
+        shown_rows, picked, full_mask.astype(jnp.float32)[None, None, :]
     ) + position_table(ground_dist, GRID, dec_width)
     all_live = jnp.full((images,), patch_count, jnp.int32)
     dec_rows, dec_state = block_forward(
         dec_in.reshape(images * patch_count, dec_width),
-        dec_full[2:],
+        dec_full,
         all_live,
         HEADS_D,
         images,
         patch_count,
     )
-    dec_again = (
-        lax.all_gather(embed_w, "fsdp", axis=0, tiled=True),
-        lax.all_gather(mask_token, "fsdp", axis=0, tiled=True),
-        lax.all_gather(dec_gain1, "fsdp", axis=0, tiled=True),
-        lax.all_gather(dec_qkv, "fsdp", axis=0, tiled=True),
-        lax.all_gather(dec_proj, "fsdp", axis=0, tiled=True),
-        lax.all_gather(dec_gain2, "fsdp", axis=0, tiled=True),
-        lax.all_gather(dec_up, "fsdp", axis=0, tiled=True),
-        lax.all_gather(dec_down, "fsdp", axis=0, tiled=True),
-    )
     d_dec = cotangent.astype(jnp.float32).reshape(images * patch_count, dec_width)
     d_dec_in, dec_grads = block_backward(
-        dec_state, d_dec, dec_again[2:], all_live, HEADS_D, images, patch_count
+        dec_state, d_dec, dec_full, all_live, HEADS_D, images, patch_count
     )
     d_positions = d_dec_in.reshape(images, patch_count, dec_width)
     grad_mask = jnp.sum(jnp.where(shown_rows, 0.0, d_positions), axis=(0, 1))
@@ -268,100 +760,55 @@
     )
     d_embed_low = d_embed.reshape(images * slot_count, dec_width).astype(jnp.bfloat16)
     grad_embed = matmul_tn(enc_low, d_embed_low)
-    d_enc = matmul_nt(d_embed_low, dec_again[0])
-    dec_shares = (
-        lax.psum_scatter(
-            grad_embed.astype(jnp.bfloat16), "fsdp", scatter_dimension=0, tiled=True
-        ).astype(jnp.float32),
-        lax.psum_scatter(
-            grad_mask.astype(jnp.bfloat16), "fsdp", scatter_dimension=0, tiled=True
-        ).astype(jnp.float32),
-        lax.psum_scatter(
-            dec_grads[0].astype(jnp.bfloat16), "fsdp", scatter_dimension=0, tiled=True
-        ).astype(jnp.float32),
-        lax.psum_scatter(
-            dec_grads[1].astype(jnp.bfloat16), "fsdp", scatter_dimension=0, tiled=True
-        ).astype(jnp.float32),
-        lax.psum_scatter(
-            dec_grads[2].astype(jnp.bfloat16), "fsdp", scatter_dimension=0, tiled=True
-        ).astype(jnp.float32),
-        lax.psum_scatter(
-            dec_grads[3].astype(jnp.bfloat16), "fsdp", scatter_dimension=0, tiled=True
-        ).astype(jnp.float32),
-        lax.psum_scatter(
-            dec_grads[4].astype(jnp.bfloat16), "fsdp", scatter_dimension=0, tiled=True
-        ).astype(jnp.float32),
-        lax.psum_scatter(
-            dec_grads[5].astype(jnp.bfloat16), "fsdp", scatter_dimension=0, tiled=True
-        ).astype(jnp.float32),
-    )
-    dec_sums = (
-        lax.psum(dec_shares[0].astype(jnp.bfloat16), "rep").astype(jnp.float32),
-        lax.psum(dec_shares[1].astype(jnp.bfloat16), "rep").astype(jnp.float32),
-        lax.psum(dec_shares[2].astype(jnp.bfloat16), "rep").astype(jnp.float32),
-        lax.psum(dec_shares[3].astype(jnp.bfloat16), "rep").astype(jnp.float32),
-        lax.psum(dec_shares[4].astype(jnp.bfloat16), "rep").astype(jnp.float32),
-        lax.psum(dec_shares[5].astype(jnp.bfloat16), "rep").astype(jnp.float32),
-        lax.psum(dec_shares[6].astype(jnp.bfloat16), "rep").astype(jnp.float32),
-        lax.psum(dec_shares[7].astype(jnp.bfloat16), "rep").astype(jnp.float32),
-    )
-    enc_again = (
-        lax.all_gather(enc_gain1, "fsdp", axis=0, tiled=True),
-        lax.all_gather(enc_qkv, "fsdp", axis=0, tiled=True),
-        lax.all_gather(enc_proj, "fsdp", axis=0, tiled=True),
-        lax.all_gather(enc_gain2, "fsdp", axis=0, tiled=True),
-        lax.all_gather(enc_up, "fsdp", axis=0, tiled=True),
-        lax.all_gather(enc_down, "fsdp", axis=0, tiled=True),
-    )
+    d_enc = matmul_nt(d_embed_low, full_embed)
     d_rows_in, enc_grads = block_backward(
-        enc_state, d_enc, enc_again, visible, HEADS, images, slot_count
-    )
-    enc_shares = (
-        lax.psum_scatter(
-            enc_grads[0].astype(jnp.bfloat16), "fsdp", scatter_dimension=0, tiled=True
-        ).astype(jnp.float32),
-        lax.psum_scatter(
-            enc_grads[1].astype(jnp.bfloat16), "fsdp", scatter_dimension=0, tiled=True
-        ).astype(jnp.float32),
-        lax.psum_scatter(
-            enc_grads[2].astype(jnp.bfloat16), "fsdp", scatter_dimension=0, tiled=True
-        ).astype(jnp.float32),
-        lax.psum_scatter(
-            enc_grads[3].astype(jnp.bfloat16), "fsdp", scatter_dimension=0, tiled=True
-        ).astype(jnp.float32),
-        lax.psum_scatter(
-            enc_grads[4].astype(jnp.bfloat16), "fsdp", scatter_dimension=0, tiled=True
-        ).astype(jnp.float32),
-        lax.psum_scatter(
-            enc_grads[5].astype(jnp.bfloat16), "fsdp", scatter_dimension=0, tiled=True
-        ).astype(jnp.float32),
-    )
-    enc_sums = (
-        lax.psum(enc_shares[0].astype(jnp.bfloat16), "rep").astype(jnp.float32),
-        lax.psum(enc_shares[1].astype(jnp.bfloat16), "rep").astype(jnp.float32),
-        lax.psum(enc_shares[2].astype(jnp.bfloat16), "rep").astype(jnp.float32),
-        lax.psum(enc_shares[3].astype(jnp.bfloat16), "rep").astype(jnp.float32),
-        lax.psum(enc_shares[4].astype(jnp.bfloat16), "rep").astype(jnp.float32),
-        lax.psum(enc_shares[5].astype(jnp.bfloat16), "rep").astype(jnp.float32),
-    )
+        enc_state, d_enc, enc_full, visible, HEADS, images, slot_count
+    )
+
+    vector_grads = (enc_grads[0], enc_grads[3], grad_mask, dec_grads[0], dec_grads[3])
+    table = jnp.concatenate([g.reshape(members, -1) for g in vector_grads], axis=1)
+    wide = 512 * -(-table.shape[1] // 512)
+    table = jnp.pad(table, ((0, 0), (0, wide - table.shape[1])))
+    table = jnp.broadcast_to(table[:, None, :], (members, 16, wide)).reshape(members * 16, wide)
+    gradients = [
+        item.astype(jnp.bfloat16)
+        for item in (
+            dec_grads[5],
+            dec_grads[4],
+            dec_grads[1],
+            dec_grads[2],
+            grad_embed,
+            enc_grads[5],
+            enc_grads[4],
+            enc_grads[2],
+            enc_grads[1],
+            table,
+        )
+    ]
+    if direct:
+        sums = reduce_all(gradients, members // 2, 1)
+    else:
+        sums = reduce_plain(gradients)
+    sums = [item.astype(jnp.float32) for item in sums]
+    small = vectors_out(sums[9], sizes)
     return (
         enc_low.reshape(images, slot_count, model_width),
         dec_rows.astype(jnp.bfloat16).reshape(images, patch_count, dec_width),
         d_rows_in.astype(jnp.bfloat16).reshape(images, slot_count, model_width),
-        enc_sums[0],
-        enc_sums[1],
-        enc_sums[2],
-        enc_sums[3],
-        enc_sums[4],
-        enc_sums[5],
-        dec_sums[0],
-        dec_sums[1],
-        dec_sums[2],
-        dec_sums[3],
-        dec_sums[4],
-        dec_sums[5],
-        dec_sums[6],
-        dec_sums[7],
+        small[0],
+        sums[8],
+        sums[7],
+        small[1],
+        sums[6],
+        sums[5],
+        sums[4],
+        small[2],
+        small[3],
+        sums[2],
+        sums[3],
+        small[4],
+        sums[1],
+        sums[0],
     )
 
 
@@ -388,7 +835,7 @@
         P(("rep", "fsdp"), None, None),
     )
     return jax.shard_map(
-        shards,
+        functools.partial(shards, dict(mesh.shape)),
         mesh=mesh,
         in_specs=placed,
         out_specs=(

time: 1010 us -> 699 us (0.69)
  waiting for transfers between devices: 527 us -> 0 us
  Pallas kernels: 0 us -> 353 us
  blocking collectives: 75.6 us -> 0 us
  matrix products: 230 us -> 192 us
  other arithmetic: 64.8 us -> 54.4 us
  local copies, waits for them, and re-layouts: 84.7 us -> 74.6 us
    pallas_call x0 -> x2, Pallas kernels: none -> 353 us  [the longest x1 194 us: reduce_all(): pl.pallas_call(functools.partial(reduce_kernel, shapes, length), out_shap...]
    reduce_scatter x9 -> x0, waiting for transfers between devices: 324 us -> none  [the longest x1 90.3 us: shards(): lax.psum_scatter(enc_grads[5].astype(jnp.bfloat16), 'fsdp', scatter_dimen...]
    all_gather x8 -> x0, waiting for transfers between devices: 141 us -> none  [the longest x1 60.1 us: shards(): lax.all_gather(enc_up, 'fsdp', axis=0, tiled=True)]
    psum x1 -> x0, waiting for transfers between devices: 57 us -> none  [shards(): lax.psum(enc_shares[1].astype(jnp.bfloat16), 'rep').astype(jnp.float32)]
    all_gather x3 -> x0, blocking collectives: 39.4 us -> none  [the longest x1 19.3 us: shards(): lax.all_gather(dec_proj, 'fsdp', axis=0, tiled=True)]
    unnamed x2 -> x0, blocking collectives: 26.4 us -> none
    dot_general x9, matrix products: 87.6 us -> 71.1 us  [matmul(): return jnp.dot(left, right, preferred_element_type=jnp.float32)]
    dot_general x9, matrix products: 58.9 us -> 47.5 us  [matmul_nt(): lax.dot_general(left, right, (((1,), (1,)), ((), ())), preferred_element_...]
  transfers between devices with their start and end apart: 18 -> 0, of which waited for: 11 -> 0; matrix products, arithmetic and copies ran while one was open for 34% -> 0% of each run, Pallas kernels for 0% -> 0%
where the time goes in v1:
time: 699 us; the launch traced here: 691 us
  Pallas kernels  353 us (51%)
  matrix products  192 us (27%)
  local copies, waits for them, and re-layouts  74.6 us (11%)
  other arithmetic  54.4 us (8%)
  between operations  15.5 us (2%)
    pallas_call x1, Pallas kernels, reduce_all(): pl.pallas_call(functools.partial(reduce_kernel, shapes, length), out_shap...  194 us
    pallas_call x1, Pallas kernels, gather_all(): pl.pallas_call(functools.partial(gather_kernel, shapes, length), out_shap...  160 us
    dot_general x9, matrix products, matmul(): return jnp.dot(left, right, preferred_element_type=jnp.float32)  71.1 us
    dot_general x9, matrix products, matmul_nt(): lax.dot_general(left, right, (((1,), (1,)), ((), ())), preferred_element_...  47.5 us
    dot_general x9, matrix products, matmul_tn(): lax.dot_general(left, right, (((0,), (0,)), ((), ())), preferred_element_...  38.9 us
    convert_element_type x9, other arithmetic, shards(): sums = [item.astype(jnp.float32) for item in sums]  16 us

profile of v1, /device:TPU:24, one launch (start us, length us, event | category | flops | bytes accessed | tf_op | source)
XLA Modules:
  0.0 691.0 jit_solution(13663147430251989963)
XLA Ops:
  14.7 159.7 %gather_all.1 = (bf16[128,512]{1,0:T(8,128)(2,1)}, bf16[1024,3072]{1,0:T(8,128)(2,1)}, bf16[1024,1024]{1,0:T(8,128)(2,1)}, bf16[1024,4096]{1,0:T(8,128)(2,1)}, b...) custom-call(bf16[16,512]{1,0:T(8,128)(2,1)} %broadcast_in_dim.225.re, ...), custom_call_target="tpu_custom_call" | custom-call | tf_op jit(solution)/shard_map/gather_all/pallas_call | solution.py:392
  178.0 8.0 %convolution_convert_fusion.3 = bf16[512,3072]{1,0:T(8,128)(2,1)} fusion(bf16[512,1024]{1,0:T(8,128)(2,1)S(1)} %fusion.63, bf16[1024,3072]{1,0:T(8,128)(2,1)} %get-tuple-element.122), kind=kOutput, calls=%fused_computation.92 | convolution fusion | flops 3222798336 | bytes 10485760 | tf_op jit(solution)/shard_map/dot_general | solution.py:20
  186.0 8.6 %reshape.868 = bf16[4,128,3,16,64]{4,3,2,1,0:T(8,128)(2,1)} reshape(bf16[512,3072]{1,0:T(8,128)(2,1)} %convolution_convert_fusion.3) | data formatting | bytes 6291456 | tf_op jit(solution)/shard_map/while/body/eval_jaxpr/reshape | solution.py:84
  194.6 6.0 fusion.121
  217.0 25.5 %multiply_convert_fusion.2 = (bf16[512,4096]{1,0:T(8,128)(2,1)S(1)}, f32[512,4096]{1,0:T(8,128)}, f32[512,4096]{1,0:T(8,128)}) fusion(bf16[1024,4096]{1,0:T(8,128)(2,1)S(1)} %bitcast.380, f32[512,1024]{1,0:T(8,128)S(1)} %get-tuple-element.256, f32[1024]{0:T(1024)S(1)} %get-tuple-element.216, f32[512]{0:T(512)S(1)} %add_rsqrt_fusion.2, ...), kind=kOutput, calls=%fused_computation.73 | convolution fusion | flops 4433379328 | bytes 31465472 | tf_op jit(solution)/shard_map/dot_general | solution.py:20
  242.5 4.5 add_convert_fusion.2
  248.0 7.6 %gather_fusion = f32[1024,512]{1,0:T(8,128)S(1)} fusion(f32[4,128,512]{2,1,0:T(8,128)S(1)} %bitcast.342, s32[1024]{0:T(1024)S(1)} %bitcast.346), kind=kCustom, calls=%fused_computation | custom fusion | bytes 4202496 | tf_op jit(solution)/shard_map/jit(take_along_axis)/gather | solution.py:734
  269.7 4.7 copy.99
  274.3 18.5 %while.4 = (s32[]{:T(128)}, bf16[2,2,256,512]{3,2,1,0:T(8,128)(2,1)}, f32[2,2,16,256]{3,2,1,0:T(8,128)S(1)}, bf16[2,2,256,1536]{2,3,1,0:T(8,128)(2,1)}, s32[]{:T(128)}) while((s32[]{:T(128)}, bf16[2,2,256,512]{3,2,1,0:T(8,128)(2,1)}, f32[2,2,16,256]{3,2,1,0:T(8,128)S(1)}, bf16[2,2,256,1536]{2,3,1,0:T(8,128)(2,1)}, s32[]{:T(128)}) %tuple.100), condition=%wide.region_11.12_spmd, body=%wide.region_8.11_spmd.sunk | while | flops 293855744 | bytes 32771152 | solution.py:68
  295.5 21.8 %multiply_convert_fusion.1 = (bf16[1024,2048]{1,0:T(8,128)(2,1)S(1)}, f32[1024,2048]{1,0:T(8,128)S(1)}, f32[1024,2048]{1,0:T(8,128)}) fusion(bf16[512,2048]{1,0:T(8,128)(2,1)S(1)} %copy-done.75, f32[1024,512]{1,0:T(8,128)S(1)} %get-tuple-element.259, f32[512]{0:T(512)S(1)} %copy-done.71, f32[1024]{0:T(1024)S(1)} %add_rsqrt_fusion, ...), kind=kOutput, calls=%fused_computation.60 | convolution fusion | flops 2285895680 | bytes 25176064 | tf_op jit(solution)/shard_map/dot_general | solution.py:20
  320.7 3.8 convolution_convert_fusion.6.refs_0_
  324.5 7.0 %fusion.32 = bf16[1024,2048]{1,0:T(8,128)(2,1)S(1)} fusion(f32[1024,2048]{1,0:T(8,128)S(1)} %get-tuple-element.201, f32[1024,2048]{1,0:T(8,128)} %get-tuple-element.260, bf16[2048,512]{1,0:T(8,128)(2,1)S(1)} %copy-done.76, bf16[1024,512]{1,0:T(8,128)(2,1)S(1)} %bitcast.361), kind=kOutput, calls=%fused_computation.57 | convolution fusion | flops 2176843776 | bytes 24117248 | tf_op jit(solution)/shard_map/dot_general | solution.py:30
  334.4 4.0 convolution_convert_fusion.5.refs_1_
  345.6 32.3 %while.5 = (s32[]{:T(128)}, bf16[2,2,256,1536]{3,2,1,0:T(8,128)(2,1)}, bf16[2,2,256,1536]{2,3,1,0:T(8,128)(2,1)}, f32[2,2,16,256]{3,2,1,0:T(8,128)S(1)}, bf16[2,2,256,512]{3,2,1,0:T(8,128)(2,1)}, /*index=5*/s32[]{:T(128)}) while((s32[]{:T(128)}, bf16[2,2,256,1536]{3,2,1,0:T(8,128)(2,1)}, bf16[2,2,256,1536]{2,3,1,0:T(8,128)(2,1)}, ...), condition=%wide.region_19.20_spmd, body=%wide.region_17.19_spmd.sunk | while | flops 705421824 | bytes 86215256 | solution.py:68
  378.0 5.4 multiply_reduce_fusion.3
  389.2 4.1 gather_fusion.1
  397.1 13.2 %add_convert_fusion = bf16[512,4096]{1,0:T(8,128)(2,1)S(1)} fusion(f32[512,4096]{1,0:T(8,128)} %get-tuple-element.205, f32[512,4096]{1,0:T(8,128)} %get-tuple-element.257, bf16[4096,1024]{1,0:T(8,128)(2,1)} %get-tuple-element.125, f32[512,1024]{1,0:T(8,128)S(1)} %fusion.115), kind=kOutput, calls=%fused_computation.59 | convolution fusion | flops 4324851712 | bytes 31457280 | tf_op jit(solution)/shard_map/dot_general | solution.py:30
  410.4 9.0 %multiply_reduce_fusion.4 = (bf16[1024]{0:T(1024)(128)(2,1)S(1)}, f32[512]{0:T(512)S(1)}, f32[512]{0:T(512)S(1)}, f32[512,1024]{1,0:T(8,128)S(1)}) fusion(f32[512,1024]{1,0:T(8,128)S(1)} %copy-done.9, f32[512]{0:T(512)S(1)} %copy-done.69, f32[512]{0:T(512)S(1)} %copy-done.58, f32[1024]{0:T(1024)S(1)} %copy-done.60, ...), kind=kOutput, calls=%fused_computation.137 | convolution fusion | flops 4299159552 | bytes 16791552 | tf_op jit(solution)/shard_map/dot_general | solution.py:30
  425.6 7.2 %convolution_convert_fusion.refs_6_ = bf16[1024,4096]{1,0:T(8,128)(2,1)} fusion(bf16[512,4096]{1,0:T(8,128)(2,1)S(1)} %copy-done.82, f32[512,1024]{1,0:T(8,128)S(1)} %copy-done.9, f32[1024]{0:T(1024)S(1)} %copy-done.60, f32[512]{0:T(512)S(1)} %copy-done.69, f32[512]{0:T(512)S(1)} %copy-done.58), kind=kOutput, calls=%fused_computation.88 | convolution fusion | flops 4301258752 | bytes 14688256 | tf_op jit(solution)/shard_map/dot_general | solution.py:24
  432.9 6.9 %convolution_convert_fusion.1.refs_5_ = bf16[4096,1024]{1,0:T(8,128)(2,1)} fusion(bf16[512,4096]{1,0:T(8,128)(2,1)S(1)} %copy-done.80, f32[512,1024]{1,0:T(8,128)S(1)} %fusion.115), kind=kOutput, calls=%fused_computation.89 | convolution fusion | flops 4299685888 | bytes 14680064 | tf_op jit(solution)/shard_map/dot_general | solution.py:24
  443.3 3.9 fusion.72
  455.7 6.2 fusion.69
  461.9 6.8 convolution_convert_fusion.2.refs_8_
  469.4 193.5 %reduce_all.1 = (bf16[256,512]{1,0:T(8,128)(2,1)}, bf16[64,2048]{1,0:T(8,128)(2,1)}, bf16[64,1536]{1,0:T(8,128)(2,1)}, bf16[64,512]{1,0:T(8,128)(2,1)}, bf16[128...) custom-call(bf16[2048,512]{1,0:T(8,128)(2,1)} %convolution_convert_f, ...), custom_call_target="tpu_custom_call" | custom-call | tf_op jit(solution)/shard_map/reduce_all/pallas_call | solution.py:637
  (338 shorter events, 156.9 us)
Async XLA Ops:
  7.2 168.2 %copy-start.2 = (bf16[4,128,1024]{2,1,0:T(8,128)(2,1)S(1)}, bf16[4,128,1024]{2,1,0:T(8,128)(2,1)}, u32[]{:S(2)}) copy-start(bf16[4,128,1024]{2,1,0:T(8,128)(2,1)} %param.23) | copy-start | bytes 3145732
  7.2 169.5 %copy-start.73 = (f32[4]{0:T(128)S(1)}, f32[4]{0:T(128)}, u32[]{:S(2)}) copy-start(f32[4]{0:T(128)} %param.40) | copy-start | bytes 52
  7.2 380.7 %sort.19.cloned.1.call-start = ((), (), s32[]{:S(2)}) async-start(), calls=%async_computation | async-start | bytes 24608 | tf_op jit(solution)/shard_map/jit(argsort)/sort | solution.py:756
  175.3 10.7 %copy-start.41 = (f32[1024]{0:T(1024)}, f32[1024]{0:T(1024)S(1)}, u32[]{:S(2)}) copy-start(f32[1024]{0:T(1024)S(1)} %get-tuple-element.217) | copy-start | bytes 12292
  175.3 41.6 %copy-start.59 = (f32[1024]{0:T(1024)}, f32[1024]{0:T(1024)S(1)}, u32[]{:S(2)}) copy-start(f32[1024]{0:T(1024)S(1)} %get-tuple-element.216) | copy-start | bytes 12292
  175.7 10.4 %copy-start.47 = (f32[512]{0:T(512)}, f32[512]{0:T(512)S(1)}, u32[]{:S(2)}) copy-start(f32[512]{0:T(512)S(1)} %get-tuple-element.239) | copy-start | bytes 6148
  176.7 9.3 %copy-start.50 = (f32[512]{0:T(512)}, f32[512]{0:T(512)S(1)}, u32[]{:S(2)}) copy-start(f32[512]{0:T(512)S(1)} %get-tuple-element.238) | copy-start | bytes 6148
  176.7 88.2 %copy-start.66 = (pred[1024]{0:T(1024)(128)(4,1)}, pred[1024]{0:T(1024)(128)(4,1)S(1)}, u32[]{:S(2)}) copy-start(pred[1024]{0:T(1024)(128)(4,1)S(1)} %broadcast_in_dim.228) | copy-start | bytes 3076
  177.6 88.5 %copy-start.53 = (f32[512]{0:T(512)}, f32[512]{0:T(512)S(1)}, u32[]{:S(2)}) copy-start(f32[512]{0:T(512)S(1)} %reshape.841) | copy-start | bytes 6148
  215.2 27.3 %slice-start.2 = ((s8[8388608]{0:T(1024)(128)(4,1)}), s8[4194304]{0:T(1024)(128)(4,1)S(1)}, s32[]{:S(2)}) async-start(s8[8388608]{0:T(1024)(128)(4,1)} %bitcast.381), calls=%async_computation.4 | async-start | bytes 8388608
  216.5 25.9 %copy-start.8 = (f32[512,1024]{1,0:T(8,128)}, f32[512,1024]{1,0:T(8,128)S(1)}, u32[]{:S(2)}) copy-start(f32[512,1024]{1,0:T(8,128)S(1)} %get-tuple-element.256) | copy-start | bytes 6291460
  216.5 25.9 %copy-start.57 = (f32[512]{0:T(512)}, f32[512]{0:T(512)S(1)}, u32[]{:S(2)}) copy-start(f32[512]{0:T(512)S(1)} %broadcast_multiply_fusion.12) | copy-start | bytes 6148
  216.9 25.5 %copy-start.68 = (f32[512]{0:T(512)}, f32[512]{0:T(512)S(1)}, u32[]{:S(2)}) copy-start(f32[512]{0:T(512)S(1)} %add_rsqrt_fusion.2) | copy-start | bytes 6148
  217.0 25.5 %slice-start.3 = ((s8[8388608]{0:T(1024)(128)(4,1)}), s8[4194304]{0:T(1024)(128)(4,1)S(1)}, s32[]{:S(2)}) async-start(s8[8388608]{0:T(1024)(128)(4,1)} %bitcast.381), calls=%async_computation.5 | async-start | bytes 8388608
  266.0 26.7 %copy-start.10 = (f32[1024,512]{1,0:T(8,128)}, f32[1024,512]{1,0:T(8,128)S(1)}, u32[]{:S(2)}) copy-start(f32[1024,512]{1,0:T(8,128)S(1)} %maximum_add_fusion) | copy-start | bytes 6291460
  295.5 21.9 %copy-start.76 = (bf16[2048,512]{1,0:T(8,128)(2,1)S(1)}, bf16[2048,512]{1,0:T(8,128)(2,1)}, u32[]{:S(2)}) copy-start(bf16[2048,512]{1,0:T(8,128)(2,1)} %get-tuple-element.131) | copy-start | bytes 6291460
  345.6 32.3 %copy-start.63 = (f32[1,2,4,128]{3,1,2,0:T(2,128)S(1)}, f32[1,2,4,128]{3,1,2,0:T(2,128)}, u32[]{:S(2)}) copy-start(f32[1,2,4,128]{3,1,2,0:T(2,128)} %copy-done.62) | copy-start | bytes 12292
  345.6 32.3 %copy-start.65 = (f32[1,2,4,128]{3,1,2,0:T(2,128)S(1)}, f32[1,2,4,128]{3,1,2,0:T(2,128)}, u32[]{:S(2)}) copy-start(f32[1,2,4,128]{3,1,2,0:T(2,128)} %copy-done.64) | copy-start | bytes 12292
  397.1 13.2 %copy-start.9 = (f32[512,1024]{1,0:T(8,128)S(1)}, f32[512,1024]{1,0:T(8,128)}, u32[]{:S(2)}) copy-start(f32[512,1024]{1,0:T(8,128)} %copy-done.8) | copy-start | bytes 6291460
  397.1 13.2 %copy-start.58 = (f32[512]{0:T(512)S(1)}, f32[512]{0:T(512)}, u32[]{:S(2)}) copy-start(f32[512]{0:T(512)} %copy-done.57) | copy-start | bytes 6148
  397.1 13.3 %copy-start.60 = (f32[1024]{0:T(1024)S(1)}, f32[1024]{0:T(1024)}, u32[]{:S(2)}) copy-start(f32[1024]{0:T(1024)} %copy-done.59) | copy-start | bytes 12292
  397.1 13.3 %copy-start.69 = (f32[512]{0:T(512)S(1)}, f32[512]{0:T(512)}, u32[]{:S(2)}) copy-start(f32[512]{0:T(512)} %copy-done.68) | copy-start | bytes 6148
  662.9 16.2 %copy-start.32 = (bf16[128,4096]{1,0:T(8,128)(2,1)S(1)}, bf16[128,4096]{1,0:T(8,128)(2,1)}, u32[]{:S(2)}) copy-start(bf16[128,4096]{1,0:T(8,128)(2,1)} %get-tuple-element.138) | copy-start | bytes 3145732
  669.3 11.3 %copy-start.31 = (bf16[512,1024]{1,0:T(8,128)(2,1)S(1)}, bf16[512,1024]{1,0:T(8,128)(2,1)}, u32[]{:S(2)}) copy-start(bf16[512,1024]{1,0:T(8,128)(2,1)} %get-tuple-element.139) | copy-start | bytes 3145732
  (66 other events, 248.8 us)
Sparse Core Ops, SparseCore 0:
  10.4 2.5 sort.21.cloned.1.call-done
  (1 shorter events, 0.0 us)

commit v2 on v1

--- a/solution.py
+++ b/solution.py
@@ -330,11 +330,11 @@
         x_step(k, s).wait_recv()
         y_step(k, s).wait_recv()
 
-        @pl.when(s % 2 == 0)
+        @pl.when((s + core) % 2 == 0)
         def _():
             d_by_y(k, s).start()
 
-        @pl.when(s % 2 == 1)
+        @pl.when((s + core) % 2 == 1)
         def _():
             d_by_x(k, s).start()
 
@@ -359,7 +359,7 @@
     for k in range(count):
         local(k).start()
         to_mate(k).start()
-    lag, total = 2, len(items)
+    lag, total = 6, len(items)
     for i in range(total + 2 * lag):
         if i < total:
             k, h, sign = items[i]
@@ -591,7 +591,7 @@
     for item in items:
         load(*item).start()
         p_step(*item).start()
-    total, lag = len(items), 2
+    total, lag = len(items), 4
     plan = [(0, stage_a), (lag, stage_b), (2 * lag, stage_c)]
     for hop in range(length - 1):
         plan.append((3 * lag - 2 + hop * lag, functools.partial(stage_z, hop=hop)))
@@ -706,26 +706,17 @@
 
     vectors = (enc_gain1, enc_gain2, mask_token, dec_gain1, dec_gain2)
     sizes = [v.shape[0] for v in vectors]
-    weights = (
-        vectors_in(vectors),
-        enc_qkv,
-        enc_proj,
-        enc_up,
-        enc_down,
-        embed_w,
-        dec_qkv,
-        dec_proj,
-        dec_up,
-        dec_down,
-    )
+    front = (vectors_in(vectors), enc_qkv, enc_proj, enc_up)
+    behind = (enc_down, embed_w, dec_qkv, dec_proj, dec_up, dec_down)
+    later = gather_plain(behind)
     if direct:
-        whole = gather_all(weights, members // 2, 0)
+        whole = gather_all(front, members // 2, 0)
     else:
-        whole = gather_plain(weights)
+        whole = gather_plain(front)
     full_gain1, full_gain2, full_mask, full_dec1, full_dec2 = vectors_out(whole[0], sizes)
-    enc_full = (full_gain1, whole[1], whole[2], full_gain2, whole[3], whole[4])
-    dec_full = (full_dec1, whole[6], whole[7], full_dec2, whole[8], whole[9])
-    full_embed = whole[5]
+    enc_full = (full_gain1, whole[1], whole[2], full_gain2, whole[3], later[0])
+    dec_full = (full_dec1, later[2], later[3], full_dec2, later[4], later[5])
+    full_embed = later[1]
 
     rows_in = patches.astype(jnp.float32).reshape(images * slot_count, model_width)
     enc_rows, enc_state = block_forward(rows_in, enc_full, visible, HEADS, images, slot_count)

time: 699 us -> 707 us (1.011)
  Pallas kernels: 353 us -> 311 us
  blocking collectives: 0 us -> 18.5 us
  matrix products: 192 us -> 210 us
  other arithmetic: 54.4 us -> 62.7 us
    pallas_call x1, Pallas kernels: 160 us -> 127 us  [gather_all(): pl.pallas_call(functools.partial(gather_kernel, shapes, length), out_shap...]
    all_gather x0 -> x1, blocking collectives: none -> 18.5 us  [gather_plain(): lax.all_gather(shard, 'fsdp', axis=0, tiled=True)]
    dot_general x9, matrix products: 71.1 us -> 82.2 us  [matmul(): return jnp.dot(left, right, preferred_element_type=jnp.float32)]
    pallas_call x1, Pallas kernels: 194 us -> 184 us  [reduce_all(): pl.pallas_call(functools.partial(reduce_kernel, shapes, length), out_shap...]
    unnamed x188 -> x178, local copies, waits for them, and re-layouts: 12.7 us -> 16.2 us
  transfers between devices with their start and end apart: 0 -> 5, of which waited for: 0 -> 0; matrix products, arithmetic and copies ran while one was open for 0% -> 24% of each run, Pallas kernels for 0% -> 18%
where the time goes in v2:
time: 707 us; the launch traced here: 701 us
  Pallas kernels  311 us (44%)
  matrix products  210 us (30%)
  local copies, waits for them, and re-layouts  78.3 us (11%)
  other arithmetic  62.7 us (9%)
  blocking collectives  18.5 us (3%)
  between operations  17.2 us (2%)
    pallas_call x1, Pallas kernels, reduce_all(): pl.pallas_call(functools.partial(reduce_kernel, shapes, length), out_shap...  184 us
    pallas_call x1, Pallas kernels, gather_all(): pl.pallas_call(functools.partial(gather_kernel, shapes, length), out_shap...  127 us
    dot_general x9, matrix products, matmul(): return jnp.dot(left, right, preferred_element_type=jnp.float32)  82.2 us
    dot_general x9, matrix products, matmul_nt(): lax.dot_general(left, right, (((1,), (1,)), ((), ())), preferred_element_...  52.4 us
    dot_general x9, matrix products, matmul_tn(): lax.dot_general(left, right, (((0,), (0,)), ((), ())), preferred_element_...  40.8 us
    all_gather x1, blocking collectives, gather_plain(): lax.all_gather(shard, 'fsdp', axis=0, tiled=True)  18.5 us
    unnamed x178, local copies, waits for them, and re-layouts  16.2 us
    convert_element_type x9, other arithmetic, shards(): sums = [item.astype(jnp.float32) for item in sums]  16 us
  transfers between devices with their start and end apart: 5, of which 0 were waited for; matrix products, arithmetic and copies ran while one was open for 24% of the time, Pallas kernels for 18%

profile of v2, /device:TPU:24, one launch (start us, length us, event | category | flops | bytes accessed | tf_op | source)
XLA Modules:
  0.0 701.2 jit_solution(11953365484894997043)
XLA Ops:
  18.8 127.1 %gather_all.1 = (bf16[128,512]{1,0:T(8,128)(2,1)}, bf16[1024,3072]{1,0:T(8,128)(2,1)}, bf16[1024,1024]{1,0:T(8,128)(2,1)}, bf16[1024,4096]{1,0:T(8,128)(2,1)}) custom-call(bf16[16,512]{1,0:T(8,128)(2,1)} %broadcast_in_dim.225.refs_0_, bf16[128,3072]{1,0:T(8,128)(2,1)} %refs_1_.1, bf16[128,1024]{1,0:T(8,128)(2,1)} %refs_2_.1, bf16[128,4096]{1,0:T(8,128)(2,1)} %refs_3_.1), custom_call_target="tpu_custom_call" | custom-call | tf_op jit(solution)/shard_map/gather_all/pallas_call | solution.py:392
  147.7 18.5 %all_gather.21 = bf16[512,512]{1,0:T(8,128)(2,1)} all-gather(bf16[64,512]{1,0:T(8,128)(2,1)S(1)} %copy-done.43), channel_id=1, replica_groups=mesh['rep'=4,'fsdp'=8] {'fsdp'}, dimensions={0}, use_global_device_ids=true | all-gather | bytes 589824 | tf_op jit(solution)/shard_map/all_gather | solution.py:669
  168.7 7.8 %convolution_convert_fusion.3 = bf16[512,3072]{1,0:T(8,128)(2,1)} fusion(bf16[512,1024]{1,0:T(8,128)(2,1)S(1)} %fusion.56, bf16[1024,3072]{1,0:T(8,128)(2,1)} %get-tuple-element.116), kind=kOutput, calls=%fused_computation.84 | convolution fusion | flops 3222798336 | bytes 10485760 | tf_op jit(solution)/shard_map/dot_general | solution.py:20
  176.5 8.7 %reshape.868 = bf16[4,128,3,16,64]{4,3,2,1,0:T(8,128)(2,1)} reshape(bf16[512,3072]{1,0:T(8,128)(2,1)} %convolution_convert_fusion.3) | data formatting | bytes 6291456 | tf_op jit(solution)/shard_map/while/body/eval_jaxpr/reshape | solution.py:84
  185.2 6.1 fusion.114
  207.0 5.4 multiply_sine_fusion.3
  212.4 5.5 multiply_sine_fusion.1
  218.0 25.5 %multiply_convert_fusion.2 = (bf16[512,4096]{1,0:T(8,128)(2,1)}, f32[512,4096]{1,0:T(8,128)}, f32[512,4096]{1,0:T(8,128)}) fusion(bf16[1024,4096]{1,0:T(8,128)(2,1)S(1)} %bitcast.361, f32[512,1024]{1,0:T(8,128)S(1)} %get-tuple-element.244, f32[1024]{0:T(1024)S(1)} %get-tuple-element.204, f32[512]{0:T(512)S(1)} %add_rsqrt_fusion.2, ...), kind=kOutput, calls=%fused_computation.65 | convolution fusion | flops 4433379328 | bytes 31465472 | tf_op jit(solution)/shard_map/dot_general | solution.py:20
  245.9 10.1 %add_convert_fusion.3 = bf16[512,1024]{1,0:T(8,128)(2,1)} fusion(f32[512,1024]{1,0:T(8,128)S(1)} %get-tuple-element.244, bf16[512,4096]{1,0:T(8,128)(2,1)} %get-tuple-element.192, bf16[4096,1024]{1,0:T(8,128)(2,1)} %all-gather.6.cloned.1.call-done), kind=kOutput, calls=%fused_computation.146 | convolution fusion | flops 4296015872 | bytes 15728640 | tf_op jit(solution)/shard_map/dot_general | solution.py:20
  258.3 7.4 %gather_fusion = f32[1024,512]{1,0:T(8,128)S(1)} fusion(f32[4,128,512]{2,1,0:T(8,128)S(1)} %bitcast.323, s32[1024]{0:T(1024)S(1)} %bitcast.327), kind=kCustom, calls=%fused_computation | custom fusion | bytes 4202496 | tf_op jit(solution)/shard_map/jit(take_along_axis)/gather | solution.py:725
  273.7 5.6 convolution_convert_fusion.4
  284.1 18.1 %while.4 = (s32[]{:T(128)}, bf16[2,2,256,512]{3,2,1,0:T(8,128)(2,1)}, f32[2,2,16,256]{3,2,1,0:T(8,128)S(1)}, bf16[2,2,256,1536]{2,3,1,0:T(8,128)(2,1)}, s32[]{:T(128)}) while((s32[]{:T(128)}, bf16[2,2,256,512]{3,2,1,0:T(8,128)(2,1)}, f32[2,2,16,256]{3,2,1,0:T(8,128)S(1)}, bf16[2,2,256,1536]{2,3,1,0:T(8,128)(2,1)}, s32[]{:T(128)}) %tuple.100), condition=%wide.region_11.12_spmd, body=%wide.region_8.11_spmd.sunk | while | flops 293855744 | bytes 32771152 | solution.py:68
  306.2 24.1 %multiply_convert_fusion.1 = (bf16[1024,2048]{1,0:T(8,128)(2,1)}, f32[1024,2048]{1,0:T(8,128)}, f32[1024,2048]{1,0:T(8,128)}) fusion(bf16[512,2048]{1,0:T(8,128)(2,1)} %all-gather.12.cloned.1.call-done, f32[1024,512]{1,0:T(8,128)} %copy-done.15, f32[512]{0:T(512)S(1)} %copy-done.70, f32[1024]{0:T(1024)S(1)} %add_rsqrt_fusion, ...), kind=kOutput, calls=%fused_computation.52 | convolution fusion | flops 2285895680 | bytes 25176064 | tf_op jit(solution)/shard_map/dot_general | solution.py:20
  330.4 8.9 %add_convert_fusion.1 = bf16[1024,2048]{1,0:T(8,128)(2,1)S(1)} fusion(f32[1024,2048]{1,0:T(8,128)} %get-tuple-element.189, f32[1024,2048]{1,0:T(8,128)} %get-tuple-element.248, bf16[1024,512]{1,0:T(8,128)(2,1)S(1)} %bitcast.341, bf16[2048,512]{1,0:T(8,128)(2,1)} %all-gather.14.cloned.1.call-done), kind=kOutput, calls=%fused_computation.51 | convolution fusion | flops 2176843776 | bytes 24117248 | tf_op jit(solution)/shard_map/dot_general | solution.py:30
  351.0 32.1 %while.5 = (s32[]{:T(128)}, bf16[2,2,256,1536]{3,2,1,0:T(8,128)(2,1)}, bf16[2,2,256,1536]{2,3,1,0:T(8,128)(2,1)}, f32[2,2,16,256]{3,2,1,0:T(8,128)S(1)}, bf16[2,2,256,512]{3,2,1,0:T(8,128)(2,1)}, /*index=5*/s32[]{:T(128)}) while((s32[]{:T(128)}, bf16[2,2,256,1536]{3,2,1,0:T(8,128)(2,1)}, bf16[2,2,256,1536]{2,3,1,0:T(8,128)(2,1)}, ...), condition=%wide.region_19.20_spmd, body=%wide.region_17.19_spmd.sunk | while | flops 705421824 | bytes 86215256 | solution.py:68
  383.1 5.4 multiply_reduce_fusion.3
  398.0 13.2 %add_convert_fusion = bf16[512,4096]{1,0:T(8,128)(2,1)S(1)} fusion(f32[512,4096]{1,0:T(8,128)} %get-tuple-element.193, f32[512,4096]{1,0:T(8,128)} %get-tuple-element.245, bf16[4096,1024]{1,0:T(8,128)(2,1)} %all-gather.6.cloned.1.call-done, f32[512,1024]{1,0:T(8,128)S(1)} %fusion.108), kind=kOutput, calls=%fused_computation.50 | convolution fusion | flops 4324851712 | bytes 31457280 | tf_op jit(solution)/shard_map/dot_general | solution.py:30
  411.3 9.0 %multiply_reduce_fusion.4 = (bf16[1024]{0:T(1024)(128)(2,1)S(1)}, f32[512]{0:T(512)S(1)}, f32[512]{0:T(512)S(1)}, f32[512,1024]{1,0:T(8,128)S(1)}) fusion(f32[512,1024]{1,0:T(8,128)S(1)} %copy-done.9, f32[512]{0:T(512)S(1)} %copy-done.69, f32[512]{0:T(512)S(1)} %copy-done.58, f32[1024]{0:T(1024)S(1)} %copy-done.60, ...), kind=kOutput, calls=%fused_computation.129 | convolution fusion | flops 4299159552 | bytes 16791552 | tf_op jit(solution)/shard_map/dot_general | solution.py:30
  426.5 7.2 %convolution_convert_fusion.refs_6_ = bf16[1024,4096]{1,0:T(8,128)(2,1)} fusion(bf16[512,4096]{1,0:T(8,128)(2,1)S(1)} %copy-done.81, f32[512,1024]{1,0:T(8,128)S(1)} %copy-done.9, f32[1024]{0:T(1024)S(1)} %copy-done.60, f32[512]{0:T(512)S(1)} %copy-done.69, f32[512]{0:T(512)S(1)} %copy-done.58), kind=kOutput, calls=%fused_computation.80 | convolution fusion | flops 4301258752 | bytes 14688256 | tf_op jit(solution)/shard_map/dot_general | solution.py:24
  433.7 6.9 convolution_convert_fusion.1.refs_5_
  458.9 5.2 convolution_convert_fusion.7.refs_2_
  467.9 8.7 %fusion.62 = (bf16[1024]{0:T(1024)(128)(2,1)S(1)}, f32[512]{0:T(512)}, f32[512]{0:T(512)}, f32[512,1024]{1,0:T(8,128)}) fusion(bf16[4,128,1024]{2,1,0:T(8,128)(2,1)S(1)} %copy-done.3, f32[512]{0:T(512)S(1)} %copy-done.53, f32[512]{0:T(512)S(1)} %copy-done.50, f32[1024]{0:T(1024)S(1)} %copy-done.45, bf16[1024,3072]{1,0:T(8,128)(2,1)} %get-tuple-element.116, ...), kind=kOutput, calls=%fused_computation.125 | convolution fusion | flops 3225942016 | bytes 12597248 | tf_op jit(solution)/shard_map/dot_general | solution.py:30
  476.7 6.8 convolution_convert_fusion.2.refs_8_
  484.1 183.6 %reduce_all.1 = (bf16[256,512]{1,0:T(8,128)(2,1)}, bf16[64,2048]{1,0:T(8,128)(2,1)}, bf16[64,1536]{1,0:T(8,128)(2,1)}, bf16[64,512]{1,0:T(8,128)(2,1)}, bf16[128...) custom-call(bf16[2048,512]{1,0:T(8,128)(2,1)} %convolution_convert_f, ...), custom_call_target="tpu_custom_call" | custom-call | tf_op jit(solution)/shard_map/reduce_all/pallas_call | solution.py:637
  (342 shorter events, 176.8 us)
Async XLA Ops:
  8.0 138.8 %copy-start.2 = (bf16[4,128,1024]{2,1,0:T(8,128)(2,1)S(1)}, bf16[4,128,1024]{2,1,0:T(8,128)(2,1)}, u32[]{:S(2)}) copy-start(bf16[4,128,1024]{2,1,0:T(8,128)(2,1)} %param.23) | copy-start | bytes 3145732
  8.0 139.5 %copy-start.74 = (f32[4]{0:T(128)S(1)}, f32[4]{0:T(128)}, u32[]{:S(2)}) copy-start(f32[4]{0:T(128)} %param.40) | copy-start | bytes 52
  8.0 139.6 %copy-start.43 = (bf16[64,512]{1,0:T(8,128)(2,1)S(1)}, bf16[64,512]{1,0:T(8,128)(2,1)}, u32[]{:S(2)}) copy-start(bf16[64,512]{1,0:T(8,128)(2,1)} %param.34) | copy-start | bytes 196612
  8.1 235.4 %sort.19.cloned.1.call-start = ((), (), s32[]{:S(2)}) async-start(), calls=%async_computation.5 | async-start | bytes 24608 | tf_op jit(solution)/shard_map/jit(argsort)/sort | solution.py:747
  8.8 237.1 %all-gather.6.cloned.1.call-start = ((), (), s32[]{:S(2)}) async-start(), calls=%async_computation | async-start | bytes 9437184 | tf_op jit(solution)/shard_map/all_gather | solution.py:669
  9.4 246.7 %all-gather.8.cloned.1.call-start = ((), (), s32[]{:S(2)}) async-start(), calls=%async_computation.1 | async-start | bytes 1179648 | tf_op jit(solution)/shard_map/all_gather | solution.py:669
  10.0 263.8 %all-gather.10.cloned.1.call-start = ((), (), s32[]{:S(2)}) async-start(), calls=%async_computation.2 | async-start | bytes 1769472 | tf_op jit(solution)/shard_map/all_gather | solution.py:669
  10.5 295.7 %all-gather.12.cloned.1.call-start = ((), (), s32[]{:S(2)}) async-start(), calls=%async_computation.3 | async-start | bytes 2359296 | tf_op jit(solution)/shard_map/all_gather | solution.py:669
  11.3 319.1 %all-gather.14.cloned.1.call-start = ((), (), s32[]{:S(2)}) async-start(), calls=%async_computation.4 | async-start | bytes 2359296 | tf_op jit(solution)/shard_map/all_gather | solution.py:669
  146.8 29.8 %copy-start.44 = (f32[1024]{0:T(1024)}, f32[1024]{0:T(1024)S(1)}, u32[]{:S(2)}) copy-start(f32[1024]{0:T(1024)S(1)} %get-tuple-element.205) | copy-start | bytes 12292
  146.8 71.2 %copy-start.59 = (f32[1024]{0:T(1024)}, f32[1024]{0:T(1024)S(1)}, u32[]{:S(2)}) copy-start(f32[1024]{0:T(1024)S(1)} %get-tuple-element.204) | copy-start | bytes 12292
  147.1 29.4 %copy-start.49 = (f32[512]{0:T(512)}, f32[512]{0:T(512)S(1)}, u32[]{:S(2)}) copy-start(f32[512]{0:T(512)S(1)} %get-tuple-element.227) | copy-start | bytes 6148
  147.5 29.0 %copy-start.52 = (f32[512]{0:T(512)}, f32[512]{0:T(512)S(1)}, u32[]{:S(2)}) copy-start(f32[512]{0:T(512)S(1)} %get-tuple-element.226) | copy-start | bytes 6148
  147.5 123.4 %copy-start.66 = (pred[1024]{0:T(1024)(128)(4,1)}, pred[1024]{0:T(1024)(128)(4,1)S(1)}, u32[]{:S(2)}) copy-start(pred[1024]{0:T(1024)(128)(4,1)S(1)} %broadcast_in_dim.228) | copy-start | bytes 3076
  166.9 106.8 %copy-start.55 = (f32[512]{0:T(512)}, f32[512]{0:T(512)S(1)}, u32[]{:S(2)}) copy-start(f32[512]{0:T(512)S(1)} %reshape.841) | copy-start | bytes 6148
  202.3 15.7 %slice-start = ((s8[8388608]{0:T(1024)(128)(4,1)}), s8[4194304]{0:T(1024)(128)(4,1)S(1)}, s32[]{:S(2)}) async-start(s8[8388608]{0:T(1024)(128)(4,1)} %bitcast.360), calls=%async_computation.7 | async-start | bytes 8388608
  202.9 15.1 %slice-start.1 = ((s8[8388608]{0:T(1024)(128)(4,1)}), s8[4194304]{0:T(1024)(128)(4,1)S(1)}, s32[]{:S(2)}) async-start(s8[8388608]{0:T(1024)(128)(4,1)} %bitcast.360), calls=%async_computation.8 | async-start | bytes 8388608
  206.6 39.3 %copy-start.8 = (f32[512,1024]{1,0:T(8,128)}, f32[512,1024]{1,0:T(8,128)S(1)}, u32[]{:S(2)}) copy-start(f32[512,1024]{1,0:T(8,128)S(1)} %get-tuple-element.244) | copy-start | bytes 6291460
  273.7 28.5 %copy-start.12 = (f32[1024,512]{1,0:T(8,128)}, f32[1024,512]{1,0:T(8,128)S(1)}, u32[]{:S(2)}) copy-start(f32[1024,512]{1,0:T(8,128)S(1)} %maximum_add_fusion) | copy-start | bytes 6291460
  306.2 24.2 %copy-start.39 = (bf16[4,256,512]{2,1,0:T(8,128)(2,1)S(1)}, bf16[4,256,512]{2,1,0:T(8,128)(2,1)}, u32[]{:S(2)}) copy-start(bf16[4,256,512]{2,1,0:T(8,128)(2,1)} %param.41) | copy-start | bytes 3145732
  351.0 32.1 %copy-start.56 = (f32[512]{0:T(512)S(1)}, f32[512]{0:T(512)}, u32[]{:S(2)}) copy-start(f32[512]{0:T(512)} %copy-done.55) | copy-start | bytes 6148
  351.0 32.1 %copy-start.63 = (f32[1,2,4,128]{3,1,2,0:T(2,128)S(1)}, f32[1,2,4,128]{3,1,2,0:T(2,128)}, u32[]{:S(2)}) copy-start(f32[1,2,4,128]{3,1,2,0:T(2,128)} %copy-done.62) | copy-start | bytes 12292
  351.0 32.1 %copy-start.65 = (f32[1,2,4,128]{3,1,2,0:T(2,128)S(1)}, f32[1,2,4,128]{3,1,2,0:T(2,128)}, u32[]{:S(2)}) copy-start(f32[1,2,4,128]{3,1,2,0:T(2,128)} %copy-done.64) | copy-start | bytes 12292
  667.7 16.2 %copy-start.38 = (bf16[128,4096]{1,0:T(8,128)(2,1)S(1)}, bf16[128,4096]{1,0:T(8,128)(2,1)}, u32[]{:S(2)}) copy-start(bf16[128,4096]{1,0:T(8,128)(2,1)} %get-tuple-element.126) | copy-start | bytes 3145732
  (66 other events, 317.1 us)
Sparse Core Ops, SparseCore 0:
  12.4 2.5 sort.21.cloned.1.call-done
  (1 shorter events, 0.0 us)
Sparse Core Ops, SparseCore 1:
  10.9 107.0 all-gather.5
  119.4 21.5 all-gather.7
  142.5 27.9 all-gather.9
  172.0 28.3 all-gather.11
  202.0 28.4 all-gather.13

commit v3 on v2

--- a/solution.py
+++ b/solution.py
@@ -1,5 +1,4 @@
 import functools
-import math
 
 import jax
 import jax.numpy as jnp
@@ -14,6 +13,7 @@
 
 
 norm_epsilon = 1e-06
+LOG2E = 1.4426950408889634
 
 
 def matmul(left, right):
@@ -59,100 +59,127 @@
     )
 
 
-def by_groups(function, members, length):
-    images = members[0].shape[0]
-    per_step = math.gcd(images, max(1, 512 // length))
-    shaped = tuple(
-        (member.reshape((images // per_step, per_step) + member.shape[1:]) for member in members)
-    )
-    results = lax.map(lambda group_items: function(*group_items), shaped)
-    return jax.tree.map(lambda result: result.reshape((images,) + result.shape[2:]), results)
-
-
-def masked_scores(queries, key_rows, live, score_scale):
-    raw_scores = (
-        jnp.einsum("nqhd,nkhd->nhqk", queries, key_rows, preferred_element_type=jnp.float32)
-        * score_scale
-    )
-    length = key_rows.shape[1]
-    valid = jnp.arange(length, dtype=jnp.int32)[None, None, None, :] < live[:, None, None, None]
-    return jnp.where(valid, raw_scores, -1e30)
-
-
-def split_heads(packed, head_count):
-    images, length, three_width = packed.shape
-    split_parts = packed.reshape(images, length, 3, head_count, three_width // (3 * head_count))
-    return (split_parts[:, :, 0], split_parts[:, :, 1], split_parts[:, :, 2])
-
-
-def attend_group(packed, live, head_count, score_scale):
-    queries, key_rows, value_rows = split_heads(packed, head_count)
-    scores = masked_scores(queries, key_rows, live, score_scale)
-    highest = jnp.max(scores, axis=-1, keepdims=True)
-    exponent = jnp.exp(scores - highest)
-    summed = jnp.sum(exponent, axis=-1, keepdims=True)
-    soft_weights = (exponent / summed).astype(jnp.bfloat16)
-    mixed_rows = jnp.einsum(
-        "nhqk,nkhd->nqhd", soft_weights, value_rows, preferred_element_type=jnp.float32
-    )
-    images, length = (packed.shape[0], packed.shape[1])
-    log_total = (highest + jnp.log(summed))[..., 0]
-    return (
-        mixed_rows.reshape(images, length, packed.shape[2] // 3).astype(jnp.bfloat16),
-        log_total,
-    )
-
-
-def attend_back_group(packed, log_total, d_mixed, live, head_count, score_scale):
-    queries, key_rows, value_rows = split_heads(packed, head_count)
-    scores = masked_scores(queries, key_rows, live, score_scale)
-    soft_float = jnp.exp(scores - log_total[..., None])
-    d_heads = d_mixed.reshape(queries.shape)
-    d_soft = jnp.einsum("nqhd,nkhd->nhqk", d_heads, value_rows, preferred_element_type=jnp.float32)
-    row_dot = jnp.sum(soft_float * d_soft, axis=-1, keepdims=True)
-    d_scores = (soft_float * (d_soft - row_dot)).astype(jnp.bfloat16)
-    d_queries = (
-        jnp.einsum("nhqk,nkhd->nqhd", d_scores, key_rows, preferred_element_type=jnp.float32)
-        * score_scale
-    )
-    d_keys = (
-        jnp.einsum("nhqk,nqhd->nkhd", d_scores, queries, preferred_element_type=jnp.float32)
-        * score_scale
-    )
-    d_values = jnp.einsum(
-        "nhqk,nqhd->nkhd",
-        soft_float.astype(jnp.bfloat16),
-        d_heads,
-        preferred_element_type=jnp.float32,
-    )
-    stacked = jnp.stack([d_queries, d_keys, d_values], axis=2)
-    return stacked.reshape(packed.shape).astype(jnp.bfloat16)
-
-
-def block_forward(rows, weights, live, head_count, images, length):
+def attend_kernel(width, heads, masked, live_ref, packed_ref, out_ref):
+    size = width // heads
+    length = packed_ref.shape[0]
+    factor = size ** (-0.5) * LOG2E
+    lanes = lax.broadcasted_iota(jnp.int32, (1, 128), 1) // size
+    live = live_ref[pl.program_id(0)]
+
+    @pl.loop(0, width // 128)
+    def _(group):
+        def part(index):
+            start = pl.multiple_of(index * width + group * 128, 128)
+            return packed_ref[:, pl.ds(start, 128)]
+
+        queries, keys, values = part(0), part(1), part(2)
+        total = None
+        for head in range(128 // size):
+            chosen = lanes == head
+            scores = factor * matmul_nt(jnp.where(chosen, queries, 0), keys)
+            if masked:
+                column = lax.broadcasted_iota(jnp.int32, (1, length), 1)
+                scores = jnp.where(column < live, scores, -1e30)
+            exponent = jnp.exp2(scores - jnp.max(scores, axis=1, keepdims=True))
+            inverse = 1.0 / jnp.sum(exponent, axis=1, keepdims=True)
+            soft = (exponent * inverse).astype(jnp.bfloat16)
+            mixed = matmul(soft, jnp.where(chosen, values, 0))
+            total = mixed if total is None else total + mixed
+        out_ref[:, pl.ds(pl.multiple_of(group * 128, 128), 128)] = total.astype(jnp.bfloat16)
+
+
+def attend_back_kernel(width, heads, masked, live_ref, packed_ref, grad_ref, out_ref):
+    size = width // heads
+    length = packed_ref.shape[0]
+    scale = size ** (-0.5)
+    lanes = lax.broadcasted_iota(jnp.int32, (1, 128), 1) // size
+    live = live_ref[pl.program_id(0)]
+
+    @pl.loop(0, width // 128)
+    def _(group):
+        def place(index):
+            return pl.ds(pl.multiple_of(index * width + group * 128, 128), 128)
+
+        queries, keys, values = (packed_ref[:, place(index)] for index in range(3))
+        d_mixed = grad_ref[:, place(0)]
+        d_queries = d_keys = d_values = None
+        for head in range(128 // size):
+            chosen = lanes == head
+            own_queries = jnp.where(chosen, queries, 0)
+            own_grad = jnp.where(chosen, d_mixed, 0)
+            own_keys = jnp.where(chosen, keys, 0)
+            scores = (scale * LOG2E) * matmul_nt(keys, own_queries)
+            if masked:
+                row = lax.broadcasted_iota(jnp.int32, (length, 1), 0)
+                scores = jnp.where(row < live, scores, -1e30)
+            exponent = jnp.exp2(scores - jnp.max(scores, axis=0, keepdims=True))
+            inverse = 1.0 / jnp.sum(exponent, axis=0, keepdims=True)
+            soft = exponent * inverse
+            d_soft = matmul_nt(values, own_grad)
+            product = soft * d_soft
+            column_dot = jnp.sum(product, axis=0, keepdims=True)
+            d_scores = (product - soft * column_dot).astype(jnp.bfloat16)
+            terms = (
+                matmul_tn(d_scores, own_keys),
+                matmul(d_scores, own_queries),
+                matmul(soft.astype(jnp.bfloat16), own_grad),
+            )
+            if d_queries is None:
+                d_queries, d_keys, d_values = terms
+            else:
+                d_queries, d_keys, d_values = (
+                    d_queries + terms[0], d_keys + terms[1], d_values + terms[2],
+                )
+        out_ref[:, place(0)] = (d_queries * scale).astype(jnp.bfloat16)
+        out_ref[:, place(1)] = (d_keys * scale).astype(jnp.bfloat16)
+        out_ref[:, place(2)] = d_values.astype(jnp.bfloat16)
+
+
+def attention_call(kernel, live, operands, width, wide, heads, masked):
+    images = live.shape[0]
+    length = operands[0].shape[0] // images
+    pairs = images * heads * length * length
+    return pl.pallas_call(
+        functools.partial(kernel, width, heads, masked),
+        out_shape=jax.ShapeDtypeStruct((images * length, wide), jnp.bfloat16),
+        grid_spec=pltpu.PrefetchScalarGridSpec(
+            num_scalar_prefetch=1,
+            grid=(images,),
+            in_specs=[
+                pl.BlockSpec((length, item.shape[1]), lambda image, live: (image, 0))
+                for item in operands
+            ],
+            out_specs=pl.BlockSpec((length, wide), lambda image, live: (image, 0)),
+        ),
+        compiler_params=pltpu.CompilerParams(vmem_limit_bytes=32 * 1024 * 1024),
+        cost_estimate=pl.CostEstimate(
+            flops=pairs * 1000,
+            transcendentals=pairs,
+            bytes_accessed=2 * images * length * (wide + 4 * width),
+        ),
+    )(live, *operands)
+
+
+def block_forward(rows, weights, live, head_count, masked):
     gain_one, w_qkv, w_out, gain_two, w_up, w_down = weights
     model_width = rows.shape[-1]
-    score_scale = (model_width // head_count) ** (-0.5)
     normal_one, inv_one = norm_stats(rows)
     normed_one = (normal_one * gain_one).astype(jnp.bfloat16)
-    packed = matmul(normed_one, w_qkv).astype(jnp.bfloat16).reshape(images, length, 3 * model_width)
-
-    def attend(group_packed, group_live):
-        return attend_group(group_packed, group_live, head_count, score_scale)
-
-    mixed_rows, log_total = by_groups(attend, (packed, live), length)
-    middle = rows + matmul(mixed_rows.reshape(images * length, model_width), w_out)
+    packed = matmul(normed_one, w_qkv).astype(jnp.bfloat16)
+    mixed_rows = attention_call(
+        attend_kernel, live, (packed,), model_width, model_width, head_count, masked
+    )
+    middle = rows + matmul(mixed_rows, w_out)
     normal_two, inv_two = norm_stats(middle)
     normed_two = (normal_two * gain_two).astype(jnp.bfloat16)
     hidden = jax.nn.gelu(matmul(normed_two, w_up), approximate=False).astype(jnp.bfloat16)
-    return (middle + matmul(hidden, w_down), (rows, packed, mixed_rows, log_total, middle))
-
-
-def block_backward(kept_state, d_out, weights, live, head_count, images, length):
-    rows, packed, mixed_rows, log_total, middle = kept_state
+    return (middle + matmul(hidden, w_down), (rows, packed, mixed_rows, middle))
+
+
+def block_backward(kept_state, d_out, weights, live, head_count, masked):
+    rows, packed, mixed_rows, middle = kept_state
     gain_one, w_qkv, w_out, gain_two, w_up, w_down = weights
     model_width = rows.shape[-1]
-    score_scale = (model_width // head_count) ** (-0.5)
     normal_two, inv_two = norm_stats(middle)
     normed_two = (normal_two * gain_two).astype(jnp.bfloat16)
     up_proj = matmul(normed_two, w_up)
@@ -167,16 +194,11 @@
     grad_gain_two = jnp.sum(d_normed_two * normal_two, axis=0)
     d_middle = d_out + norm_back(d_normed_two * gain_two, normal_two, inv_two)
     d_attn = d_middle.astype(jnp.bfloat16)
-    grad_out = matmul_tn(mixed_rows.reshape(images * length, model_width), d_attn)
-    d_mixed = matmul_nt(d_attn, w_out).astype(jnp.bfloat16).reshape(images, length, model_width)
-
-    def attend_back(group_packed, group_total, group_grad, group_live):
-        return attend_back_group(
-            group_packed, group_total, group_grad, group_live, head_count, score_scale
-        )
-
-    d_packed = by_groups(attend_back, (packed, log_total, d_mixed, live), length)
-    d_packed = d_packed.reshape(images * length, 3 * model_width)
+    grad_out = matmul_tn(mixed_rows, d_attn)
+    d_mixed = matmul_nt(d_attn, w_out).astype(jnp.bfloat16)
+    d_packed = attention_call(
+        attend_back_kernel, live, (packed, d_mixed), model_width, 3 * model_width, head_count, masked
+    )
     normal_one, inv_one = norm_stats(rows)
     normed_one = (normal_one * gain_one).astype(jnp.bfloat16)
     grad_qkv = matmul_tn(normed_one, d_packed)
@@ -706,20 +728,20 @@
 
     vectors = (enc_gain1, enc_gain2, mask_token, dec_gain1, dec_gain2)
     sizes = [v.shape[0] for v in vectors]
-    front = (vectors_in(vectors), enc_qkv, enc_proj, enc_up)
-    behind = (enc_down, embed_w, dec_qkv, dec_proj, dec_up, dec_down)
-    later = gather_plain(behind)
+    front = (vectors_in(vectors), enc_qkv, enc_proj, enc_up, enc_down, dec_proj)
     if direct:
         whole = gather_all(front, members // 2, 0)
     else:
         whole = gather_plain(front)
     full_gain1, full_gain2, full_mask, full_dec1, full_dec2 = vectors_out(whole[0], sizes)
-    enc_full = (full_gain1, whole[1], whole[2], full_gain2, whole[3], later[0])
-    dec_full = (full_dec1, later[2], later[3], full_dec2, later[4], later[5])
-    full_embed = later[1]
+    behind = lax.optimization_barrier((embed_w, dec_qkv, dec_up, dec_down, whole[0]))
+    later = gather_plain(behind[:4])
+    enc_full = (full_gain1, whole[1], whole[2], full_gain2, whole[3], whole[4])
+    dec_full = (full_dec1, later[1], whole[5], full_dec2, later[2], later[3])
+    full_embed = later[0]
 
     rows_in = patches.astype(jnp.float32).reshape(images * slot_count, model_width)
-    enc_rows, enc_state = block_forward(rows_in, enc_full, visible, HEADS, images, slot_count)
+    enc_rows, enc_state = block_forward(rows_in, enc_full, visible, HEADS, True)
     enc_low = enc_rows.astype(jnp.bfloat16)
     embedded = matmul(enc_low, full_embed).reshape(images, slot_count, dec_width)
     picked = jnp.take_along_axis(
@@ -735,12 +757,11 @@
         dec_full,
         all_live,
         HEADS_D,
-        images,
-        patch_count,
+        False,
     )
     d_dec = cotangent.astype(jnp.float32).reshape(images * patch_count, dec_width)
     d_dec_in, dec_grads = block_backward(
-        dec_state, d_dec, dec_full, all_live, HEADS_D, images, patch_count
+        dec_state, d_dec, dec_full, all_live, HEADS_D, False
     )
     d_positions = d_dec_in.reshape(images, patch_count, dec_width)
     grad_mask = jnp.sum(jnp.where(shown_rows, 0.0, d_positions), axis=(0, 1))
@@ -753,7 +774,7 @@
     grad_embed = matmul_tn(enc_low, d_embed_low)
     d_enc = matmul_nt(d_embed_low, full_embed)
     d_rows_in, enc_grads = block_backward(
-        enc_state, d_enc, enc_full, visible, HEADS, images, slot_count
+        enc_state, d_enc, enc_full, visible, HEADS, True
     )
 
     vector_grads = (enc_grads[0], enc_grads[3], grad_mask, dec_grads[0], dec_grads[3])

time: 707 us -> 634 us (0.90)
  Pallas kernels: 311 us -> 361 us
  local copies, waits for them, and re-layouts: 78.3 us -> 38.3 us
  matrix products: 210 us -> 174 us
  other arithmetic: 62.7 us -> 36.6 us
  blocking collectives: 18.5 us -> 0 us
    pallas_call x0 -> x4, Pallas kernels: none -> 79.7 us  [attention_call(): pl.pallas_call(functools.partial(kernel, width, heads, masked), out_shape...]
    dot_general x20 -> x0, matrix products: 34.7 us -> none  [the longest x5 8.41 us: masked_scores(): jnp.einsum('nqhd,nkhd->nhqk', queries, key_rows, preferred_element_type=j...]
    pallas_call x1, Pallas kernels: 127 us -> 97.1 us  [gather_all(): pl.pallas_call(functools.partial(gather_kernel, shapes, length), out_shap...]
    all_gather x1 -> x0, blocking collectives: 18.5 us -> none  [gather_plain(): lax.all_gather(shard, 'fsdp', axis=0, tiled=True)]
    reshape x3 -> x0, local copies, waits for them, and re-layouts: 11.9 us -> none  [the longest x1 8.66 us: split_heads(): packed.reshape(images, length, 3, head_count, three_width // (3 * head_co...]
    dynamic_slice x8 -> x0, local copies, waits for them, and re-layouts: 8.62 us -> none  [by_groups(): results = lax.map(lambda group_items: function(*group_items), shaped)]
    unnamed x178 -> x147, local copies, waits for them, and re-layouts: 16.2 us -> 7.73 us
  transfers between devices with their start and end apart: 5 -> 4, of which waited for: 0 -> 0; matrix products, arithmetic and copies ran while one was open for 24% -> 18% of each run, Pallas kernels for 18% -> 5%
where the time goes in v3:
time: 634 us; the launch traced here: 629 us
  Pallas kernels  361 us (57%)
  matrix products  174 us (27%)
  local copies, waits for them, and re-layouts  38.3 us (6%)
  other arithmetic  36.6 us (6%)
  between operations  16.8 us (3%)
    pallas_call x1, Pallas kernels, reduce_all(): pl.pallas_call(functools.partial(reduce_kernel, shapes, length), out_shap...  184 us
    pallas_call x1, Pallas kernels, gather_all(): pl.pallas_call(functools.partial(gather_kernel, shapes, length), out_shap...  97.1 us
    dot_general x9, matrix products, matmul(): return jnp.dot(left, right, preferred_element_type=jnp.float32)  82.8 us
    pallas_call x4, Pallas kernels, attention_call(): pl.pallas_call(functools.partial(kernel, width, heads, masked), out_shape...  79.7 us
    dot_general x9, matrix products, matmul_nt(): lax.dot_general(left, right, (((1,), (1,)), ((), ())), preferred_element_...  50.8 us
    dot_general x9, matrix products, matmul_tn(): lax.dot_general(left, right, (((0,), (0,)), ((), ())), preferred_element_...  40.8 us
    gather x1, local copies, waits for them, and re-layouts, shards(): jnp.take_along_axis(embedded, jnp.minimum(unshuffle, slot_count - 1)[:, :...  12.7 us
  transfers between devices with their start and end apart: 4, of which 0 were waited for; matrix products, arithmetic and copies ran while one was open for 18% of the time, Pallas kernels for 5%

profile of v3, /device:TPU:24, one launch (start us, length us, event | category | flops | bytes accessed | tf_op | source)
XLA Modules:
  0.0 629.1 jit_solution(10123386924816593519)
XLA Ops:
  12.9 97.1 %gather_all.1 = (bf16[128,512]{1,0:T(8,128)(2,1)}, bf16[1024,3072]{1,0:T(8,128)(2,1)}, bf16[1024,1024]{1,0:T(8,128)(2,1)}, bf16[1024,4096]{1,0:T(8,128)(2,1)}, b...) custom-call(bf16[16,512]{1,0:T(8,128)(2,1)} %broadcast_in_dim.66.refs_0_, bf16[128,3072]{1,0:T(8,128)(2,1)} %refs_1_.1, ...), custom_call_target="tpu_custom_call" | custom-call | tf_op jit(solution)/shard_map/gather_all/pallas_call | solution.py:414
  114.1 6.8 %convolution_convert_fusion.3.packed_ref = bf16[512,3072]{1,0:T(8,128)(2,1)S(1)} fusion(bf16[512,1024]{1,0:T(8,128)(2,1)S(1)} %fusion.26, bf16[1024,3072]{1,0:T(8,128)(2,1)} %get-tuple-element.39), kind=kOutput, calls=%fused_computation.47 | convolution fusion | flops 3222798336 | bytes 10485760 | tf_op jit(solution)/shard_map/dot_general | solution.py:20
  120.9 16.0 %shard_map.314 = bf16[512,1024]{1,0:T(8,128)(2,1)S(1)} custom-call(s32[4]{0:T(128)S(1)} %copy-done.6, bf16[512,3072]{1,0:T(8,128)(2,1)S(1)} %convolution_convert_fusion.3.packed_ref), custom_call_target="tpu_custom_call" | custom-call | flops 1048576000 | bytes 5242880 | tf_op jit(solution)/shard_map/pallas_call | solution.py:142
  140.0 27.6 %multiply_convert_fusion.1 = (bf16[512,4096]{1,0:T(8,128)(2,1)S(1)}, f32[512,4096]{1,0:T(8,128)}, f32[512,4096]{1,0:T(8,128)}) fusion(bf16[1024,4096]{1,0:T(8,128)(2,1)} %get-tuple-element.41, f32[512,1024]{1,0:T(8,128)} %copy-done.18, f32[1024]{0:T(1024)S(1)} %get-tuple-element.80, f32[512]{0:T(512)S(1)} %add_rsqrt_fusion.1, ...), kind=kOutput, calls=%fused_computation.29 | convolution fusion | flops 4433379328 | bytes 31465472 | tf_op jit(solution)/shard_map/dot_general | solution.py:20
  167.5 9.7 %add_convert_fusion.2 = bf16[512,1024]{1,0:T(8,128)(2,1)} fusion(f32[512,1024]{1,0:T(8,128)S(1)} %copy-done.19, bf16[512,4096]{1,0:T(8,128)(2,1)S(1)} %get-tuple-element.75, bf16[4096,1024]{1,0:T(8,128)(2,1)} %get-tuple-element.42), kind=kOutput, calls=%fused_computation.88 | convolution fusion | flops 4296015872 | bytes 15728640 | tf_op jit(solution)/shard_map/dot_general | solution.py:20
  181.5 5.6 multiply_sine_fusion.3
  190.8 12.7 %gather_fusion = f32[1024,512]{1,0:T(8,128)} fusion(f32[4,128,512]{2,1,0:T(8,128)S(1)} %bitcast.165, s32[1024]{0:T(1024)S(1)} %bitcast.166), kind=kCustom, calls=%fused_computation | custom fusion | bytes 4202496 | tf_op jit(solution)/shard_map/jit(take_along_axis)/gather | solution.py:747
  212.4 17.6 %shard_map.315 = bf16[1024,512]{1,0:T(8,128)(2,1)S(1)} custom-call(s32[4]{0:T(128)S(1)} %broadcast_75_live_ref.2.live_ref, bf16[1024,1536]{1,0:T(8,128)(2,1)S(1)} %convolution_convert_fusion.4.packed_ref), custom_call_target="tpu_custom_call" | custom-call | flops 4194304000 | bytes 5242880 | tf_op jit(solution)/shard_map/pallas_call | solution.py:142
  234.2 24.1 %multiply_convert_fusion = (bf16[1024,2048]{1,0:T(8,128)(2,1)}, f32[1024,2048]{1,0:T(8,128)}, f32[1024,2048]{1,0:T(8,128)}) fusion(bf16[512,2048]{1,0:T(8,128)(2,1)} %all-gather.9.cloned.1.call-done, f32[1024,512]{1,0:T(8,128)} %get-tuple-element.115, f32[512]{0:T(512)S(1)} %reshape.488, f32[1024]{0:T(1024)S(1)} %add_rsqrt_fusion, ...), kind=kOutput, calls=%fused_computation.16 | convolution fusion | flops 2285895680 | bytes 25176064 | tf_op jit(solution)/shard_map/dot_general | solution.py:20
  258.3 9.3 %fusion.7 = bf16[1024,2048]{1,0:T(8,128)(2,1)S(1)} fusion(f32[1024,2048]{1,0:T(8,128)} %get-tuple-element.74, f32[1024,2048]{1,0:T(8,128)} %get-tuple-element.116, bf16[2048,512]{1,0:T(8,128)(2,1)} %all-gather.11.cloned.1.call-done, bf16[1024,512]{1,0:T(8,128)(2,1)S(1)} %bitcast.170), kind=kOutput, calls=%fused_computation.13 | convolution fusion | flops 2176843776 | bytes 24117248 | tf_op jit(solution)/shard_map/dot_general | solution.py:30
  267.6 5.9 multiply_reduce_fusion
  278.4 28.8 %shard_map.316 = bf16[1024,1536]{1,0:T(8,128)(2,1)S(1)} custom-call(s32[4]{0:T(128)S(1)} %broadcast_75_live_ref.2.live_ref, bf16[1024,1536]{1,0:T(8,128)(2,1)S(1)} %copy-done.8, bf16[1024,512]{1,0:T(8,128)(2,1)S(1)} %convolution_convert_fusion.11.grad_ref), custom_call_target="tpu_custom_call" | custom-call | flops 4194304000 | bytes 7340032 | tf_op jit(solution)/shard_map/pallas_call | solution.py:142
  311.4 9.9 %gather_fusion.1 = bf16[512,512]{1,0:T(8,128)(2,1)} fusion(bf16[4,256,512]{2,1,0:T(8,128)(2,1)} %bitcast.169, s32[512]{0:T(512)S(1)} %fusion.46), kind=kCustom, calls=%fused_computation.1 | custom fusion | bytes 1052672 | tf_op jit(solution)/shard_map/jit(take_along_axis)/gather | solution.py:771
  323.5 14.7 %add_convert_fusion = bf16[512,4096]{1,0:T(8,128)(2,1)} fusion(f32[512,4096]{1,0:T(8,128)} %get-tuple-element.76, f32[512,4096]{1,0:T(8,128)} %get-tuple-element.113, bf16[4096,1024]{1,0:T(8,128)(2,1)} %get-tuple-element.42, f32[512,1024]{1,0:T(8,128)S(1)} %fusion.56), kind=kOutput, calls=%fused_computation.15 | convolution fusion | flops 4324851712 | bytes 31457280 | tf_op jit(solution)/shard_map/dot_general | solution.py:30
  338.2 8.8 %multiply_reduce_fusion.2 = (bf16[1024]{0:T(1024)(128)(2,1)S(1)}, f32[512]{0:T(512)S(1)}, f32[512]{0:T(512)S(1)}, f32[512,1024]{1,0:T(8,128)S(1)}) fusion(f32[512,1024]{1,0:T(8,128)S(1)} %copy-done.20, f32[512]{0:T(512)S(1)} %add_rsqrt_fusion.1, f32[512]{0:T(512)S(1)} %broadcast_multiply_fusion.12, f32[1024]{0:T(1024)S(1)} %get-tuple-element.80, ...), kind=kOutput, calls=%fused_computation.75 | convolution fusion | flops 4299159552 | bytes 16791552 | tf_op jit(solution)/shard_map/dot_general | solution.py:30
  351.3 17.3 %shard_map.317 = bf16[512,3072]{1,0:T(8,128)(2,1)S(1)} custom-call(s32[4]{0:T(128)S(1)} %copy-done.6, bf16[512,3072]{1,0:T(8,128)(2,1)S(1)} %copy-done.1, bf16[512,1024]{1,0:T(8,128)(2,1)S(1)} %convolution_convert_fusion.9.grad_ref), custom_call_target="tpu_custom_call" | custom-call | flops 1048576000 | bytes 7340032 | tf_op jit(solution)/shard_map/pallas_call | solution.py:142
  368.7 5.6 fusion.32
  374.3 5.6 convolution_convert_fusion.2.refs_8_
  382.6 7.4 %convolution_convert_fusion.refs_6_ = bf16[1024,4096]{1,0:T(8,128)(2,1)} fusion(bf16[512,4096]{1,0:T(8,128)(2,1)S(1)} %copy-done.67, f32[512,1024]{1,0:T(8,128)S(1)} %copy-done.20, f32[1024]{0:T(1024)S(1)} %get-tuple-element.80, f32[512]{0:T(512)S(1)} %add_rsqrt_fusion.1, f32[512]{0:T(512)S(1)} %broadcast_multiply_fusion.12), kind=kOutput, calls=%fused_computation.44 | convolution fusion | flops 4301258752 | bytes 14688256 | tf_op jit(solution)/shard_map/dot_general | solution.py:24
  390.0 7.1 %convolution_convert_fusion.1.refs_5_ = bf16[4096,1024]{1,0:T(8,128)(2,1)} fusion(bf16[512,4096]{1,0:T(8,128)(2,1)S(1)} %copy-done.66, f32[512,1024]{1,0:T(8,128)S(1)} %fusion.56), kind=kOutput, calls=%fused_computation.45 | convolution fusion | flops 4299685888 | bytes 14680064 | tf_op jit(solution)/shard_map/dot_general | solution.py:24
  403.9 5.7 convolution_convert_fusion.5.refs_1_
  409.9 5.9 convolution_convert_fusion.6.refs_0_
  416.5 184.2 %reduce_all.1 = (bf16[256,512]{1,0:T(8,128)(2,1)}, bf16[64,2048]{1,0:T(8,128)(2,1)}, bf16[64,1536]{1,0:T(8,128)(2,1)}, bf16[64,512]{1,0:T(8,128)(2,1)}, bf16[128...) custom-call(bf16[2048,512]{1,0:T(8,128)(2,1)} %convolution_convert_f, ...), custom_call_target="tpu_custom_call" | custom-call | tf_op jit(solution)/shard_map/reduce_all/pallas_call | solution.py:659
  616.4 4.9 add_convert_fusion.1
  (241 shorter events, 73.9 us)
Async XLA Ops:
  8.0 103.9 %copy-start.43 = (s32[4,256]{1,0:T(4,128)S(1)}, s32[4,256]{1,0:T(4,128)}, u32[]{:S(2)}) copy-start(s32[4,256]{1,0:T(4,128)} %param.35) | copy-start | bytes 12292
  8.0 104.9 %copy-start.15 = (bf16[4,128,1024]{2,1,0:T(8,128)(2,1)S(1)}, bf16[4,128,1024]{2,1,0:T(8,128)(2,1)}, u32[]{:S(2)}) copy-start(bf16[4,128,1024]{2,1,0:T(8,128)(2,1)} %param.19) | copy-start | bytes 3145732
  8.0 179.0 %sort.19.cloned.1.call-start = ((), (), s32[]{:S(2)}) async-start(), calls=%async_computation.4 | async-start | bytes 24608 | tf_op jit(solution)/shard_map/jit(argsort)/sort | solution.py:768
  8.8 179.7 %all-gather.5.cloned.1.call-start = ((), (), s32[]{:S(2)}) async-start(), calls=%async_computation | async-start | bytes 1179648 | tf_op jit(solution)/shard_map/all_gather | solution.py:691
  12.9 100.7 %copy-start.6 = (s32[4]{0:T(128)S(1)}, s32[4]{0:T(128)}, u32[]{:S(2)}) copy-start(s32[4]{0:T(128)} %live_ref.3) | copy-start | bytes 52
  110.0 98.4 %all-gather.7.cloned.1.call-start = ((), (), s32[]{:S(2)}) async-start(), calls=%async_computation.1 | async-start | bytes 1769472 | tf_op jit(solution)/shard_map/all_gather | solution.py:691
  110.6 123.6 %all-gather.9.cloned.1.call-start = ((), (), s32[]{:S(2)}) async-start(), calls=%async_computation.2 | async-start | bytes 2359296 | tf_op jit(solution)/shard_map/all_gather | solution.py:691
  111.2 147.1 %all-gather.11.cloned.1.call-start = ((), (), s32[]{:S(2)}) async-start(), calls=%async_computation.3 | async-start | bytes 2359296 | tf_op jit(solution)/shard_map/all_gather | solution.py:691
  120.9 17.4 %copy-start = (bf16[512,3072]{1,0:T(8,128)(2,1)}, bf16[512,3072]{1,0:T(8,128)(2,1)S(1)}, u32[]{:S(2)}) copy-start(bf16[512,3072]{1,0:T(8,128)(2,1)S(1)} %convolution_convert_fusion.3.packed_ref) | copy-start | bytes 9437188
  140.0 27.6 %copy-start.19 = (f32[512,1024]{1,0:T(8,128)S(1)}, f32[512,1024]{1,0:T(8,128)}, u32[]{:S(2)}) copy-start(f32[512,1024]{1,0:T(8,128)} %copy-done.18) | copy-start | bytes 6291460
  208.4 21.7 %copy-start.11 = (f32[1024,512]{1,0:T(8,128)}, f32[1024,512]{1,0:T(8,128)S(1)}, u32[]{:S(2)}) copy-start(f32[1024,512]{1,0:T(8,128)S(1)} %maximum_add_fusion) | copy-start | bytes 6291460
  212.4 17.6 %copy-start.7 = (bf16[1024,1536]{1,0:T(8,128)(2,1)}, bf16[1024,1536]{1,0:T(8,128)(2,1)S(1)}, u32[]{:S(2)}) copy-start(bf16[1024,1536]{1,0:T(8,128)(2,1)S(1)} %convolution_convert_fusion.4.packed_ref) | copy-start | bytes 9437188
  212.4 17.6 %copy-start.24 = (bf16[512,512]{1,0:T(8,128)(2,1)S(1)}, bf16[512,512]{1,0:T(8,128)(2,1)}, u32[]{:S(2)}) copy-start(bf16[512,512]{1,0:T(8,128)(2,1)} %get-tuple-element.45) | copy-start | bytes 1572868
  234.2 24.2 %copy-start.34 = (bf16[4,256,512]{2,1,0:T(8,128)(2,1)S(1)}, bf16[4,256,512]{2,1,0:T(8,128)(2,1)}, u32[]{:S(2)}) copy-start(bf16[4,256,512]{2,1,0:T(8,128)(2,1)} %param.37) | copy-start | bytes 3145732
  275.7 33.9 %copy-start.9 = (f32[1024,512]{1,0:T(8,128)}, f32[1024,512]{1,0:T(8,128)S(1)}, u32[]{:S(2)}) copy-start(f32[1024,512]{1,0:T(8,128)S(1)} %multiply_add_fusion.2) | copy-start | bytes 6291460
  278.4 28.9 %copy-start.12 = (f32[1024,512]{1,0:T(8,128)S(1)}, f32[1024,512]{1,0:T(8,128)}, u32[]{:S(2)}) copy-start(f32[1024,512]{1,0:T(8,128)} %copy-done.11) | copy-start | bytes 6291460
  278.4 28.9 %copy-start.60 = (bf16[512,1536]{1,0:T(8,128)(2,1)S(1)}, bf16[512,1536]{1,0:T(8,128)(2,1)}, u32[]{:S(2)}) copy-start(bf16[512,1536]{1,0:T(8,128)(2,1)} %all-gather.7.cloned.1.call-done) | copy-start | bytes 4718596
  347.0 21.6 %slice-start = ((s8[6291456]{0:T(1024)(128)(4,1)}), s8[2097152]{0:T(1024)(128)(4,1)S(1)}, s32[]{:S(2)}) async-start(s8[6291456]{0:T(1024)(128)(4,1)} %bitcast.190), calls=%async_computation.6 | async-start | bytes 4194304
  348.6 31.3 %copy-start.21 = (f32[512,1024]{1,0:T(8,128)}, f32[512,1024]{1,0:T(8,128)S(1)}, u32[]{:S(2)}) copy-start(f32[512,1024]{1,0:T(8,128)S(1)} %multiply_add_fusion) | copy-start | bytes 6291460
  348.6 20.0 %slice-start.1 = ((s8[6291456]{0:T(1024)(128)(4,1)}), s8[4194304]{0:T(1024)(128)(4,1)S(1)}, s32[]{:S(2)}) async-start(s8[6291456]{0:T(1024)(128)(4,1)} %bitcast.190), calls=%async_computation.7 | async-start | bytes 8388608
  351.3 17.3 %copy-start.16 = (bf16[4,128,1024]{2,1,0:T(8,128)(2,1)S(1)}, bf16[4,128,1024]{2,1,0:T(8,128)(2,1)}, u32[]{:S(2)}) copy-start(bf16[4,128,1024]{2,1,0:T(8,128)(2,1)} %param.19) | copy-start | bytes 3145732
  351.3 17.4 %copy-start.45 = (f32[1024]{0:T(1024)S(1)}, f32[1024]{0:T(1024)}, u32[]{:S(2)}) copy-start(f32[1024]{0:T(1024)} %copy-done.44) | copy-start | bytes 12292
  351.3 17.4 %copy-start.48 = (f32[512]{0:T(512)S(1)}, f32[512]{0:T(512)}, u32[]{:S(2)}) copy-start(f32[512]{0:T(512)} %copy-done.47) | copy-start | bytes 6148
  351.3 17.4 %copy-start.51 = (f32[512]{0:T(512)S(1)}, f32[512]{0:T(512)}, u32[]{:S(2)}) copy-start(f32[512]{0:T(512)} %copy-done.50) | copy-start | bytes 6148
  (51 other events, 256.1 us)
Sparse Core Ops, SparseCore 0:
  12.3 2.6 sort.21.cloned.1.call-done
  (1 shorter events, 0.0 us)
Sparse Core Ops, SparseCore 1:
  110.1 20.8 all-gather.4
  132.5 24.6 all-gather.6
  158.6 28.4 all-gather.8
  188.6 28.4 all-gather.10
